TPU v7x, 256 devices: a whole 4x4x8 slice. The times are simulated.
256 devices in a mesh: col: 32 (over x, z_hi, core), row: 8 (over y, z_lo).
Axes of the slice: x: 4, y: 4, z: 8 (z_hi: 4, z_lo: 2; z = z_hi * 2 + z_lo), core: 2. Of those that a mesh axis runs over, the one named last changes fastest.
Arguments:
- weight: bfloat16 [8192, 53248], P('row', 'col'), may hold values from -6 to 6
- factor: float32 [1664, 53248], P('row', 'col'), may hold values from -1 to 2, as said below
- keep_mask: int32 [64, 13], P('row'), may hold values 0 or 1
Outputs:
- pruned: bfloat16 [8192, 53248], P('row', 'col')
Inputs may be any that keep to these rules, and one draw needn't show every extreme that they name: factor[i, k] = 0 for k < i; the diagonal entries factor[i, i] lie in [0.5, 2].
All inputs are finite; a program needn't handle non-finite values. No bound on the sum of `keep_mask` on one device may be relied on, other than what follows from the above.
Results may differ from a plain program's by a relative error of at most 0.0035.
Values may be sent and summed in bfloat16 or wider, within the bound.
No kernel may reach another device: no remote copies, remote signals or barrier semaphores. Data moves between devices by JAX's collectives and lax.ppermute only.
A program may use at most 192 MiB of HBM per device.

v0:
```python
import jax
import jax.numpy as jnp
from jax import lax
from jax.experimental import pallas as pl
from jax.experimental.pallas import tpu as pltpu
from jax.sharding import PartitionSpec as P


BLK = 128
PCOLS = 1664
LANES = 8
LANE_ROWS = 208
STRIP_BLOCKS = 3
PAD = 256
NBLK = PCOLS // BLK
ROWS_DEV = 1024
QUARTER = 256
HALF = 128
BF = jnp.bfloat16
F32 = jnp.float32


def split(a):
    high = a.astype(BF)
    return high, (a - high.astype(F32)).astype(BF)


def mm_split(a, b):
    right = jnp.concatenate(split(b), axis=1)
    left = jnp.concatenate(split(a), axis=1)
    both = jnp.dot(left, jnp.concatenate([right, right], axis=0), preferred_element_type=F32)
    return both[:, :BLK] + both[:, BLK:]


def triangle_inverses(fulls):
    row = lax.broadcasted_iota(jnp.int32, (BLK, BLK), 0)
    column = lax.broadcasted_iota(jnp.int32, (BLK, BLK), 1)
    eye = (row == column).astype(F32)
    stricts, pivots = [], []
    for full in fulls:
        on_diag = jnp.where(row == column, full, 0.0)
        pivots.append(jnp.sum(on_diag, axis=0, keepdims=True))
        stricts.append(jnp.where(column > row, full, 0.0) / jnp.sum(on_diag, axis=1, keepdims=True))
    nears = [jnp.where((row // 8) == (column // 8), strict, 0.0) for strict in stricts]
    near2s = [mm_split(near, near) for near in nears]
    near4s = [mm_split(near2, near2) for near2 in near2s]
    inverses = [mm_split(eye - near, eye + near2) for near, near2 in zip(nears, near2s)]
    inverses = [mm_split(inverse, eye + near4) for inverse, near4 in zip(inverses, near4s)]
    width = 8
    while width < BLK:
        pair = 2 * width
        inside = ((row // pair) == (column // pair)) & ((row // width) != (column // width))
        offs = [jnp.where(inside, strict, 0.0) for strict in stricts]
        steps = [mm_split(off, inverse) for off, inverse in zip(offs, inverses)]
        inverses = [inverse - mm_split(inverse, step) for inverse, step in zip(inverses, steps)]
        width = pair
    return [inverse / pivot for inverse, pivot in zip(inverses, pivots)]


def local_kernel(lane_ref, factor_ref, payload_ref, low_ref, rows_ref, inverse_ref):
    lane = lane_ref[0]
    first = jnp.minimum(lane * LANE_ROWS // BLK, NBLK - STRIP_BLOCKS)
    low = factor_ref[...].astype(BF)
    payload_ref[:, :PCOLS] = low
    low_ref[...] = low
    start = pl.multiple_of(first * BLK, BLK)
    rows_ref[PAD : PAD + LANE_ROWS, :] = factor_ref[:, pl.ds(start, STRIP_BLOCKS * BLK)]
    row = lax.broadcasted_iota(jnp.int32, (BLK, BLK), 0)
    column = lax.broadcasted_iota(jnp.int32, (BLK, BLK), 1)
    eye = (row == column).astype(F32)
    fulls, places = [], []
    for place in range(STRIP_BLOCKS):
        shift = (first + place) * BLK - lane * LANE_ROWS
        at = pl.multiple_of(shift + PAD, 16)
        valid = (row + shift >= 0) & (row + shift < LANE_ROWS)
        block = rows_ref[pl.ds(at, BLK), place * BLK : (place + 1) * BLK]
        fulls.append(jnp.where(valid, block, eye))
        places.append((at, valid))
    for (at, valid), inverse in zip(places, triangle_inverses(fulls)):
        here = inverse_ref[pl.ds(at, BLK), :]
        inverse_ref[pl.ds(at, BLK), :] = jnp.where(valid, inverse, here)
    high, lowpart = split(inverse_ref[PAD : PAD + LANE_ROWS, :])
    payload_ref[:, PCOLS : PCOLS + BLK] = high
    payload_ref[:, PCOLS + BLK :] = lowpart


def local_part(lane, factor):
    vmem = pl.BlockSpec(memory_space=pltpu.VMEM)
    smem = pl.BlockSpec(memory_space=pltpu.SMEM)
    return pl.pallas_call(
        local_kernel,
        in_specs=[smem, vmem],
        out_specs=(vmem, vmem),
        out_shape=(
            jax.ShapeDtypeStruct((LANE_ROWS, PCOLS + 2 * BLK), BF),
            jax.ShapeDtypeStruct((LANE_ROWS, PCOLS), BF),
        ),
        scratch_shapes=[
            pltpu.VMEM((PAD + LANE_ROWS + PAD, STRIP_BLOCKS * BLK), F32),
            pltpu.VMEM((PAD + LANE_ROWS + PAD, BLK), F32),
        ],
        name="local_part",
    )(lane, factor)


def prune_kernel(keep_ref, order_ref, weight_ref, *rest):
    pieces = rest[:LANES]
    quarter_refs = rest[LANES : LANES + 4]
    kept_ref, factor_ref, errors_ref = rest[LANES + 4 :]
    for place in range(LANES):
        start = pl.multiple_of(order_ref[place] * LANE_ROWS, 16)
        factor_ref[pl.ds(start, LANE_ROWS), :] = pieces[place][...]
    row = lax.broadcasted_iota(jnp.int32, (BLK, BLK), 0)
    column = lax.broadcasted_iota(jnp.int32, (BLK, BLK), 1)
    eye = (row == column).astype(F32)
    for block in range(NBLK):
        at = block * BLK
        edge = (at // LANE_ROWS + 1) * LANE_ROWS - at
        if edge < BLK:
            stored = factor_ref[at : at + BLK, PCOLS:]
            whole = stored[:, :BLK].astype(F32) + stored[:, BLK:].astype(F32)
            top = jnp.where(row < edge, whole, eye)
            bottom = jnp.where(row < edge, eye, whole)
            factor_ref[at : at + BLK, PCOLS:] = jnp.concatenate(split(mm_split(top, bottom)), axis=1)
    for low in range(0, PCOLS, 2 * BLK):
        width = min(2 * BLK, PCOLS - low)
        current = weight_ref[:, low : low + width].astype(F32)
        if low:
            current = current - jnp.dot(
                errors_ref[:, :low], factor_ref[:low, low : low + width], preferred_element_type=F32
            )
        for half in range(width // BLK):
            at = low + half * BLK
            part = current[:, half * BLK : (half + 1) * BLK]
            if half:
                part = part - jnp.dot(
                    errors_ref[:, low : low + BLK],
                    factor_ref[low : low + BLK, at : at + BLK],
                    preferred_element_type=F32,
                )
            high, lowpart = split(part)
            right = factor_ref[at : at + BLK, PCOLS:]
            both = jnp.dot(
                jnp.concatenate([high, lowpart], axis=1),
                jnp.concatenate([right, right], axis=0),
                preferred_element_type=F32,
            )
            solved = (both[:, :BLK] + both[:, BLK:]).astype(BF)
            for group in range(ROWS_DEV // BLK):
                top = group * BLK
                keep = keep_ref[group, at // BLK] > 0
                error = jnp.where(keep, jnp.zeros((BLK, BLK), BF), solved[top : top + BLK])
                errors_ref[top : top + BLK, at : at + BLK] = error
                inner = top % QUARTER
                quarter_refs[top // QUARTER][inner : inner + BLK, at : at + BLK] = error
                kept_ref[top : top + BLK, at : at + BLK] = jnp.where(
                    keep, high[top : top + BLK], jnp.zeros((BLK, BLK), BF)
                )


def prune(keep_mask, order, weight, pieces):
    vmem = pl.BlockSpec(memory_space=pltpu.VMEM)
    smem = pl.BlockSpec(memory_space=pltpu.SMEM)
    quarter = jax.ShapeDtypeStruct((QUARTER, PCOLS), BF)
    return pl.pallas_call(
        prune_kernel,
        in_specs=[smem, smem, vmem] + [vmem] * LANES,
        out_specs=(vmem,) * 5,
        out_shape=(quarter,) * 4 + (jax.ShapeDtypeStruct((ROWS_DEV, PCOLS), BF),),
        scratch_shapes=[
            pltpu.VMEM((PCOLS, PCOLS + 2 * BLK), BF),
            pltpu.VMEM((ROWS_DEV, PCOLS), BF),
        ],
        name="prune",
    )(keep_mask, order, weight, *pieces)


def subtract(piece, factor, weight_ref, kept_ref, owner):
    product = jnp.dot(piece, factor, preferred_element_type=F32)
    trailing = (weight_ref[...].astype(F32) - product).astype(BF)
    return jnp.where(owner > 0, kept_ref[...], trailing)


def own_kernel(at_ref, piece_ref, *rest):
    parts = rest[:5]
    weight_ref, kept_ref, out_ref, factor_ref = rest[5:]
    for place, part in enumerate(parts):
        start = pl.multiple_of(at_ref[2 + place] * LANE_ROWS, 16)
        factor_ref[pl.ds(start, part.shape[0]), :] = part[...]
    out_ref[...] = subtract(piece_ref[...], factor_ref[...], weight_ref, kept_ref, at_ref[1])


def near_kernel(at_ref, first_ref, second_ref, factor_ref, weight_ref, kept_ref, out_ref):
    for step, piece_ref in enumerate((first_ref, second_ref)):

        @pl.when(pl.program_id(0) == step)
        def _():
            out_ref[...] = subtract(piece_ref[...], factor_ref[...], weight_ref, kept_ref, at_ref[2])


def far_kernel(at_ref, first_ref, second_ref, factor_ref, weight_ref, kept_ref, out_ref, piece_ref):
    for place, half_ref in enumerate((first_ref, second_ref)):
        start = pl.multiple_of(at_ref[2 + place] * HALF, HALF)
        piece_ref[pl.ds(start, HALF), :] = half_ref[...]
    out_ref[...] = subtract(piece_ref[...], factor_ref[...], weight_ref, kept_ref, at_ref[1])


def finish(kernel, steps, at, inputs, weight, kept, extra=None, scratch=()):
    block = pl.BlockSpec((QUARTER, PCOLS), lambda i, at_ref: (at_ref[i], 0))
    vmem = pl.BlockSpec(memory_space=pltpu.VMEM)
    out_shape = [jax.ShapeDtypeStruct((ROWS_DEV, PCOLS), BF)]
    if extra is not None:
        out_shape.append(extra)
    return pl.pallas_call(
        kernel,
        grid_spec=pltpu.PrefetchScalarGridSpec(
            num_scalar_prefetch=1,
            grid=(steps,),
            in_specs=[vmem] * len(inputs) + [block, block],
            out_specs=[block] + [vmem] * (len(out_shape) - 1),
            scratch_shapes=list(scratch),
        ),
        out_shape=out_shape,
        input_output_aliases={len(inputs) + 2: 0},
    )(at, *inputs, weight, kept)


def col_at(x, zh, core):
    return (x % 4) * 8 + (zh % 4) * 2 + core


def row_at(y, zl):
    return (y % 4) * 2 + zl


def vector(value):
    return jnp.reshape(value, (1,)).astype(jnp.int32)


def per_device(weight, factor, keep_mask):
    section = lax.axis_index("col")
    lane = lax.axis_index("row")
    x_at = section // 8
    zh_at = (section // 2) % 4
    core_at = section % 2
    payload, factor_low = local_part(vector(lane), factor)

    def hop(array, dy, flip):
        pairs = [(row_at(y, zl), row_at(y + dy, zl ^ flip)) for y in range(4) for zl in (0, 1)]
        return lax.ppermute(array, ("col", "row"), pairs)

    y_at, zl_at = lane // 2, lane % 2
    up_same = hop(payload, 1, 0)
    down_other = hop(payload, 3, 1)
    up_other = hop(payload, 1, 1)
    down_same = hop(payload, 3, 0)
    other = hop(payload, 0, 1)
    far_same = hop(up_same, 1, 0)
    far_other = hop(down_other, 3, 0)
    pieces = [payload, up_same, down_other, up_other, down_same, other, far_same, far_other]
    order = [
        lane,
        row_at(y_at + 3, zl_at),
        row_at(y_at + 1, 1 - zl_at),
        row_at(y_at + 3, 1 - zl_at),
        row_at(y_at + 1, zl_at),
        row_at(y_at, 1 - zl_at),
        row_at(y_at + 2, zl_at),
        row_at(y_at + 2, 1 - zl_at),
    ]
    *quarters, kept = prune(keep_mask, jnp.stack(order).astype(jnp.int32), weight, pieces)

    def along(array, dy):
        return lax.ppermute(array, "row", [(row_at(y, zl), row_at(y + dy, zl)) for y in range(4) for zl in (0, 1)])

    partner = lax.ppermute(factor_low, "row", [(k, k ^ 1) for k in range(LANES)])
    even = zl_at == 0
    pair = jnp.concatenate(
        [jnp.where(even, factor_low, partner), jnp.where(even, partner, factor_low)], axis=0
    )
    pair_up = along(pair, 1)
    pair_down = along(pair, 3)
    far_even = along(pair_up[:LANE_ROWS], 1)
    far_odd = along(pair_down[LANE_ROWS:], 3)
    parts = (pair, pair_up, pair_down, far_even, far_odd)
    part_rows = [
        row_at(y_at, 0), row_at(y_at + 3, 0), row_at(y_at + 1, 0), row_at(y_at + 2, 0), row_at(y_at + 2, 1)
    ]

    got = None
    for k in (2, 1, 3):
        sent = lax.ppermute(quarters[k], "col", [(0, col_at(k, 0, 0))])
        got = sent if got is None else got + sent
    own = jnp.where(x_at == 0, quarters[0], got)
    up = lax.ppermute(own, "col", [(col_at(x, 0, 0), col_at(x, 1, 0)) for x in range(4)])
    down = lax.ppermute(own, "col", [(col_at(x, 0, 0), col_at(x, 3, 0)) for x in range(4)])
    far_a = lax.ppermute(up[:HALF], "col", [(col_at(x, 1, 0), col_at(x, 2, 0)) for x in range(4)])
    far_b = lax.ppermute(down[HALF:], "col", [(col_at(x, 3, 0), col_at(x, 2, 0)) for x in range(4)])
    own = jnp.where(zh_at == 0, own, up + down + jnp.concatenate([far_a, far_b], axis=0))

    places = [(x, z) for x in range(4) for z in range(4)]
    share = [(col_at(x, z, 0), col_at(x, z, 1)) for x, z in places]
    swap = [(col_at(x, z, c), col_at(x, z, 1 - c)) for x, z in places for c in (0, 1)]
    ring = [(col_at(x, z, 0), col_at(x + 1, z, 0)) for x, z in places]
    ring += [(col_at(x, z, 1), col_at(x - 1, z, 1)) for x, z in places]
    shared = lax.ppermute(own, "col", share)
    own = jnp.where(core_at == 0, own, shared)
    near = lax.ppermute(own, "col", ring)
    far = lax.ppermute(lax.dynamic_slice(near, (core_at * HALF, 0), (HALF, PCOLS)), "col", ring)
    near_other = lax.ppermute(near, "col", swap)
    far_other = lax.ppermute(far, "col", swap)

    def ints(*values):
        return jnp.stack(values).astype(jnp.int32)

    owner = section == 0
    factor_shape = jax.ShapeDtypeStruct((PCOLS, PCOLS), BF)
    out, factor_all = finish(own_kernel, 1, ints(x_at, owner, *part_rows), (own, *parts), weight, kept, factor_shape)
    ways = ints((x_at + 3 - 2 * core_at) % 4, (x_at + 1 + 2 * core_at) % 4, owner)
    (out,) = finish(near_kernel, 2, ways, (near, near_other, factor_all), weight, out)
    (out,) = finish(
        far_kernel,
        1,
        ints((x_at + 2) % 4, owner, core_at, 1 - core_at),
        (far, far_other, factor_all),
        weight,
        out,
        scratch=[pltpu.VMEM((QUARTER, PCOLS), BF)],
    )
    return out


def solution(mesh):
    in_specs = (P("row", "col"), P("row", "col"), P("row", None))
    out_specs = P("row", "col")
    return jax.shard_map(per_device, mesh=mesh, in_specs=in_specs, out_specs=out_specs, check_vma=False)
```

profile of v0, /device:TPU:1, one launch (start us, length us, event | category | flops | bytes accessed | tf_op | source)
XLA Modules:
  0.0 179.5 jit_solution(1386780775524870825)
XLA Ops:
  0.0 4.8 %local_part.1 = (bf16[208,1920]{1,0:T(8,128)(2,1)}, bf16[208,1664]{1,0:T(8,128)(2,1)}) custom-call(s32[1]{0:T(128)} %bitcast.4.lane_ref, f32[208,1664]{1,0:T(8,128)} %factor_ref.1), custom_call_target="tpu_custom_call" | custom-call | tf_op jit(solution)/shard_map/local_part/pallas_call | solution.py:90
  7.6 1.6 collective-permute-start.4
  9.2 1.5 collective-permute-start.5
  10.7 1.7 collective-permute-start.6
  14.2 15.4 %prune.1 = (bf16[256,1664]{1,0:T(8,128)(2,1)}, bf16[256,1664]{1,0:T(8,128)(2,1)}, bf16[256,1664]{1,0:T(8,128)(2,1)}, bf16[256,1664]{1,0:T(8,128)(2,1)}, bf16[1024,1664]{1,0:T(8,128)(2,1)}) custom-call(s32[8,13]{1,0:T(8,128)} %keep_ref.1, s32[8]{0:T(128)} %stack.91.order_ref, bf16[1024,1664]{1,0:T(8,128)(2,1)} %weight_ref.5, ...), custom_call_target="tpu_custom_call" | custom-call | tf_op jit(solution)/shard_map/prune/pallas_call | solution.py:165
  31.8 1.3 add_select_fusion
  34.7 1.4 collective-permute-start.12
  36.1 1.4 collective-permute-start.13
  37.6 2.5 %collective-permute-start.18 = (bf16[208,1664]{1,0:T(8,128)(2,1)}, bf16[208,1664]{1,0:T(8,128)(2,1)}, u32[]{:S(2)}, u32[]{:S(2)}) collective-permute-start(bf16[208,1664]{1,0:T(8,128)(2,1)} %get-tuple-element.19), channel_id=1, source_target_pairs={{0,1},{1,0},{2,3},{3,2},{4,5},{5,4},{6,7},{7,6},{8,9},{9,8},{10,11... | collective-permute-start | bytes 2076680 | tf_op jit(solution)/shard_map/ppermute | solution.py:276
  40.0 1.6 fusion
  42.9 7.8 %collective-permute-done.18 = bf16[208,1664]{1,0:T(8,128)(2,1)} collective-permute-done((bf16[208,1664]{1,0:T(8,128)(2,1)}, bf16[208,1664]{1,0:T(8,128)(2,1)}, u32[]{:S(2)}, u32[]{:S(2)}) %collective-permute-start.18) | collective-permute-done | bytes 692256 | tf_op jit(solution)/shard_map/ppermute | solution.py:276
  50.7 1.4 broadcast_select_fusion.2
  52.6 2.7 %collective-permute-start.20 = (bf16[416,1664]{1,0:T(8,128)(2,1)S(1)}, bf16[416,1664]{1,0:T(8,128)(2,1)}, u32[]{:S(2)}, u32[]{:S(2)}) collective-permute-start(bf16[416,1664]{1,0:T(8,128)(2,1)S(1)} %pad_maximum_fusion.rest_0_), channel_id=1, source_target_pairs={{0,6},{1,7},{2,0},{3,1},{4,2},{5,3},{6,4},{7,5},{8,14},{9,15},{10,... | collective-permute-start | bytes 4153352 | tf_op jit(solution)/shard_map/ppermute | solution.py:274
  55.2 56.5 %collective-permute-done.14 = bf16[256,1664]{1,0:T(8,128)(2,1)} collective-permute-done((bf16[256,1664]{1,0:T(8,128)(2,1)S(1)}, bf16[256,1664]{1,0:T(8,128)(2,1)}, u32[]{:S(2)}, u32[]{:S(2)}) %collective-permute-start.14) | collective-permute-done | bytes 852000 | tf_op jit(solution)/shard_map/ppermute | solution.py:306
  113.1 11.9 %collective-permute-done.15.first_ref = bf16[256,1664]{1,0:T(8,128)(2,1)S(1)} collective-permute-done((bf16[256,1664]{1,0:T(8,128)(2,1)S(1)}, bf16[256,1664]{1,0:T(8,128)(2,1)S(1)}, u32[]{:S(2)}, u32[]{:S(2)}) %collective-permute-start.15) | collective-permute-done | bytes 852000 | tf_op jit(solution)/shard_map/ppermute | solution.py:308
  125.0 11.6 %collective-permute-start.23 = (bf16[256,1664]{1,0:T(8,128)(2,1)S(1)}, bf16[256,1664]{1,0:T(8,128)(2,1)}, u32[]{:S(2)}, u32[]{:S(2)}) collective-permute-start(bf16[256,1664]{1,0:T(8,128)(2,1)S(1)} %collective-permute-done.15.first_ref), channel_id=1, source_target_pairs={{0,8},{8,0},{16,24},{24,16},{32,40},{40,32},{48,56},{56,48},{64,72... | collective-permute-start | bytes 2555912 | tf_op jit(solution)/shard_map/ppermute | solution.py:310
  136.8 2.0 %slice.18 = bf16[208,1664]{1,0:T(8,128)(2,1)} slice(bf16[416,1664]{1,0:T(8,128)(2,1)} %collective-permute-done.19.rest_1_), slice={[0:208], [0:1664]} | slice | bytes 1384448 | tf_op jit(solution)/shard_map/slice | solution.py:283
  140.0 2.8 %collective-permute-start.22 = (bf16[208,1664]{1,0:T(8,128)(2,1)S(1)}, bf16[208,1664]{1,0:T(8,128)(2,1)S(1)}, u32[]{:S(2)}, u32[]{:S(2)}) collective-permute-start(bf16[208,1664]{1,0:T(8,128)(2,1)S(1)} %slice.19), channel_id=1, source_target_pairs={{0,6},{1,7},{2,0},{3,1},{4,2},{5,3},{6,4},{7,5},{8,14},{9,15},{10,... | collective-permute-start | bytes 2076680 | tf_op jit(solution)/shard_map/ppermute | solution.py:274
  142.7 1.4 collective-permute-done.16.first_ref
  144.1 2.1 %collective-permute-start.17 = (bf16[128,1664]{1,0:T(8,128)(2,1)}, bf16[128,1664]{1,0:T(8,128)(2,1)S(1)}, u32[]{:S(2)}, u32[]{:S(2)}) collective-permute-start(bf16[128,1664]{1,0:T(8,128)(2,1)} %collective-permute-done.16.first_ref), channel_id=1, source_target_pairs={{0,8},{8,0},{16,24},{24,16},{32,40},{40,32},{48,56},{56,48},{64,72... | collective-permute-start | bytes 1277960 | tf_op jit(solution)/shard_map/ppermute | solution.py:311
  148.2 7.0 %collective-permute-done.21.rest_3_ = bf16[208,1664]{1,0:T(8,128)(2,1)} collective-permute-done((bf16[208,1664]{1,0:T(8,128)(2,1)}, bf16[208,1664]{1,0:T(8,128)(2,1)}, u32[]{:S(2)}, u32[]{:S(2)}) %collective-permute-start.21) | collective-permute-done | bytes 692256 | tf_op jit(solution)/shard_map/ppermute | solution.py:274
  156.0 7.1 %shard_map.37 = (bf16[1024,1664]{1,0:T(8,128)(2,1)}, bf16[1664,1664]{1,0:T(8,128)(2,1)}) custom-call(s32[7]{0:T(128)} %stack.98.at_ref, bf16[256,1664]{1,0:T(8,128)(2,1)} %copy-done.1, bf16[416,1664]{1,0:T(8,128)(2,1)} %copy-done, bf16[416,1664]{1,0:T(8,128)(2,1)} %collective-permute-done.19.rest_1_, ...), custom_call_target="tpu_custom_call", output_to_operand_aliasing={{0}: (8, {})} | custom-call | tf_op jit(solution)/shard_map/pallas_call | solution.py:214
  163.1 8.9 %shard_map.38.kept_ref = bf16[1024,1664]{1,0:T(8,128)(2,1)} custom-call(s32[3]{0:T(128)} %pad_add_fusion.1.at_ref, bf16[256,1664]{1,0:T(8,128)(2,1)} %copy-done.2, bf16[256,1664]{1,0:T(8,128)(2,1)} %collective-permute-done.23.second_ref, bf16[1664,1664]{1,0:T(8,128)(2,1)} %get-tuple-element.21.factor_ref, ...), custom_call_target="tpu_custom_call", output_to_operand_aliasing={{}: (5, {})} | custom-call | tf_op jit(solution)/shard_map/pallas_call | solution.py:214
  172.8 6.7 %shard_map.39 = bf16[1024,1664]{1,0:T(8,128)(2,1)} custom-call(s32[4]{0:T(128)} %pad_add_fusion.at_ref, bf16[128,1664]{1,0:T(8,128)(2,1)} %collective-permute-done.16.first_ref, bf16[128,1664]{1,0:T(8,128)(2,1)} %copy-done.8, bf16[1664,1664]{1,0:T(8,128)(2,1)} %get-tuple-element.21.factor_ref, ...), custom_call_target="tpu_custom_call", output_to_operand_aliasing={{}: (5, {})} | custom-call | tf_op jit(solution)/shard_map/pallas_call | solution.py:214
  (61 shorter events, 16.2 us)
Async XLA Ops:
  4.8 4.4 %collective-permute-start = (bf16[208,1920]{1,0:T(8,128)(2,1)}, bf16[208,1920]{1,0:T(8,128)(2,1)S(1)}, u32[]{:S(2)}, u32[]{:S(2)}) collective-permute-start(bf16[208,1920]{1,0:T(8,128)(2,1)} %get-tuple-element.14.rest_0_), channel_id=1, source_target_pairs={{0,2},{1,3},{2,4},{3,5},{4,6},{5,7},{6,0},{7,1}} | collective-permute-start | bytes 2396168 | tf_op jit(solution)/shard_map/ppermute | solution.py:250
  5.5 5.3 %collective-permute-start.1 = (bf16[208,1920]{1,0:T(8,128)(2,1)}, bf16[208,1920]{1,0:T(8,128)(2,1)S(1)}, u32[]{:S(2)}, u32[]{:S(2)}) collective-permute-start(bf16[208,1920]{1,0:T(8,128)(2,1)} %get-tuple-element.14.rest_0_), channel_id=1, source_target_pairs={{0,7},{1,6},{2,1},{3,0},{4,3},{5,2},{6,5},{7,4}} | collective-permute-start | bytes 2396168 | tf_op jit(solution)/shard_map/ppermute | solution.py:250
  6.2 6.8 %collective-permute-start.2 = (bf16[208,1920]{1,0:T(8,128)(2,1)}, bf16[208,1920]{1,0:T(8,128)(2,1)S(1)}, u32[]{:S(2)}, u32[]{:S(2)}) collective-permute-start(bf16[208,1920]{1,0:T(8,128)(2,1)} %get-tuple-element.14.rest_0_), channel_id=1, source_target_pairs={{0,3},{1,2},{2,5},{3,4},{4,7},{5,6},{6,1},{7,0}} | collective-permute-start | bytes 2396168 | tf_op jit(solution)/shard_map/ppermute | solution.py:250
  6.9 6.1 %collective-permute-start.3 = (bf16[208,1920]{1,0:T(8,128)(2,1)}, bf16[208,1920]{1,0:T(8,128)(2,1)S(1)}, u32[]{:S(2)}, u32[]{:S(2)}) collective-permute-start(bf16[208,1920]{1,0:T(8,128)(2,1)} %get-tuple-element.14.rest_0_), channel_id=1, source_target_pairs={{0,6},{1,7},{2,0},{3,1},{4,2},{5,3},{6,4},{7,5}} | collective-permute-start | bytes 2396168 | tf_op jit(solution)/shard_map/ppermute | solution.py:250
  7.6 5.4 %collective-permute-start.4 = (bf16[208,1920]{1,0:T(8,128)(2,1)}, bf16[208,1920]{1,0:T(8,128)(2,1)}, u32[]{:S(2)}, u32[]{:S(2)}) collective-permute-start(bf16[208,1920]{1,0:T(8,128)(2,1)} %get-tuple-element.14.rest_0_), channel_id=1, source_target_pairs={{0,1},{1,0},{2,3},{3,2},{4,5},{5,4},{6,7},{7,6}} | collective-permute-start | bytes 2396168 | tf_op jit(solution)/shard_map/ppermute | solution.py:250
  9.2 3.9 %collective-permute-start.5 = (bf16[208,1920]{1,0:T(8,128)(2,1)S(1)}, bf16[208,1920]{1,0:T(8,128)(2,1)}, u32[]{:S(2)}, u32[]{:S(2)}) collective-permute-start(bf16[208,1920]{1,0:T(8,128)(2,1)S(1)} %collective-permute-done.rest_1_), channel_id=1, source_target_pairs={{0,2},{1,3},{2,4},{3,5},{4,6},{5,7},{6,0},{7,1}} | collective-permute-start | bytes 2396168 | tf_op jit(solution)/shard_map/ppermute | solution.py:250
  10.7 2.3 %collective-permute-start.6 = (bf16[208,1920]{1,0:T(8,128)(2,1)S(1)}, bf16[208,1920]{1,0:T(8,128)(2,1)}, u32[]{:S(2)}, u32[]{:S(2)}) collective-permute-start(bf16[208,1920]{1,0:T(8,128)(2,1)S(1)} %collective-permute-done.1.rest_2_), channel_id=1, source_target_pairs={{0,6},{1,7},{2,0},{3,1},{4,2},{5,3},{6,4},{7,5}} | collective-permute-start | bytes 2396168 | tf_op jit(solution)/shard_map/ppermute | solution.py:250
  29.6 2.2 %collective-permute-start.7 = (bf16[256,1664]{1,0:T(8,128)(2,1)}, bf16[256,1664]{1,0:T(8,128)(2,1)S(1)}, u32[]{:S(2)}, u32[]{:S(2)}) collective-permute-start(bf16[256,1664]{1,0:T(8,128)(2,1)} %get-tuple-element.16), channel_id=1, source_target_pairs={{0,128},{1,129},{2,130},{3,131},{4,132},{5,133},{6,134},{7,135}} | collective-permute-start | bytes 2555912 | tf_op jit(solution)/shard_map/ppermute | solution.py:292
  30.3 1.5 collective-permute-start.8
  31.1 0.8 collective-permute-start.9
  33.2 1.4 collective-permute-start.10
  33.9 2.2 %collective-permute-start.11 = (bf16[256,1664]{1,0:T(8,128)(2,1)S(1)}, bf16[256,1664]{1,0:T(8,128)(2,1)S(1)}, u32[]{:S(2)}, u32[]{:S(2)}) collective-permute-start(bf16[256,1664]{1,0:T(8,128)(2,1)S(1)} %add_select_fusion), channel_id=1, source_target_pairs={{0,48},{64,112},{128,176},{192,240},{1,49},{65,113},{129,177},{193... | collective-permute-start | bytes 2555912 | tf_op jit(solution)/shard_map/ppermute | solution.py:296
  34.7 5.4 %collective-permute-start.12 = (bf16[128,1664]{1,0:T(8,128)(2,1)S(1)}, bf16[128,1664]{1,0:T(8,128)(2,1)}, u32[]{:S(2)}, u32[]{:S(2)}) collective-permute-start(bf16[128,1664]{1,0:T(8,128)(2,1)S(1)} %slice.16), channel_id=1, source_target_pairs={{16,32},{80,96},{144,160},{208,224},{17,33},{81,97},{145,161},{209... | collective-permute-start | bytes 1277960 | tf_op jit(solution)/shard_map/ppermute | solution.py:297
  36.1 3.9 %collective-permute-start.13 = (bf16[128,1664]{1,0:T(8,128)(2,1)S(1)}, bf16[128,1664]{1,0:T(8,128)(2,1)}, u32[]{:S(2)}, u32[]{:S(2)}) collective-permute-start(bf16[128,1664]{1,0:T(8,128)(2,1)S(1)} %slice.17), channel_id=1, source_target_pairs={{48,32},{112,96},{176,160},{240,224},{49,33},{113,97},{177,161},{2... | collective-permute-start | bytes 1277960 | tf_op jit(solution)/shard_map/ppermute | solution.py:298
  37.6 13.2 %collective-permute-start.18 = (bf16[208,1664]{1,0:T(8,128)(2,1)}, bf16[208,1664]{1,0:T(8,128)(2,1)}, u32[]{:S(2)}, u32[]{:S(2)}) collective-permute-start(bf16[208,1664]{1,0:T(8,128)(2,1)} %get-tuple-element.19), channel_id=1, source_target_pairs={{0,1},{1,0},{2,3},{3,2},{4,5},{5,4},{6,7},{7,6},{8,9},{9,8},{10,11... | collective-permute-start | bytes 2076680 | tf_op jit(solution)/shard_map/ppermute | solution.py:276
  41.6 70.1 %collective-permute-start.14 = (bf16[256,1664]{1,0:T(8,128)(2,1)S(1)}, bf16[256,1664]{1,0:T(8,128)(2,1)}, u32[]{:S(2)}, u32[]{:S(2)}) collective-permute-start(bf16[256,1664]{1,0:T(8,128)(2,1)S(1)} %fusion), channel_id=1, source_target_pairs={{0,8},{16,24},{32,40},{48,56},{64,72},{80,88},{96,104},{112,120},{... | collective-permute-start | bytes 2555912 | tf_op jit(solution)/shard_map/ppermute | solution.py:306
  52.3 84.5 %collective-permute-start.19 = (bf16[416,1664]{1,0:T(8,128)(2,1)S(1)}, bf16[416,1664]{1,0:T(8,128)(2,1)}, u32[]{:S(2)}, u32[]{:S(2)}) collective-permute-start(bf16[416,1664]{1,0:T(8,128)(2,1)S(1)} %pad_maximum_fusion.rest_0_), channel_id=1, source_target_pairs={{0,2},{1,3},{2,4},{3,5},{4,6},{5,7},{6,0},{7,1},{8,10},{9,11},{10,... | collective-permute-start | bytes 4153352 | tf_op jit(solution)/shard_map/ppermute | solution.py:274
  52.6 86.2 %collective-permute-start.20 = (bf16[416,1664]{1,0:T(8,128)(2,1)S(1)}, bf16[416,1664]{1,0:T(8,128)(2,1)}, u32[]{:S(2)}, u32[]{:S(2)}) collective-permute-start(bf16[416,1664]{1,0:T(8,128)(2,1)S(1)} %pad_maximum_fusion.rest_0_), channel_id=1, source_target_pairs={{0,6},{1,7},{2,0},{3,1},{4,2},{5,3},{6,4},{7,5},{8,14},{9,15},{10,... | collective-permute-start | bytes 4153352 | tf_op jit(solution)/shard_map/ppermute | solution.py:274
  113.0 12.0 %collective-permute-start.15 = (bf16[256,1664]{1,0:T(8,128)(2,1)S(1)}, bf16[256,1664]{1,0:T(8,128)(2,1)S(1)}, u32[]{:S(2)}, u32[]{:S(2)}) collective-permute-start(bf16[256,1664]{1,0:T(8,128)(2,1)S(1)} %broadcast_select_fusion.piece_ref), channel_id=1, source_target_pairs={{0,64},{16,80},{32,96},{48,112},{64,128},{80,144},{96,160},{112,17... | collective-permute-start | bytes 2555912 | tf_op jit(solution)/shard_map/ppermute | solution.py:308
  125.0 38.1 %collective-permute-start.23 = (bf16[256,1664]{1,0:T(8,128)(2,1)S(1)}, bf16[256,1664]{1,0:T(8,128)(2,1)}, u32[]{:S(2)}, u32[]{:S(2)}) collective-permute-start(bf16[256,1664]{1,0:T(8,128)(2,1)S(1)} %collective-permute-done.15.first_ref), channel_id=1, source_target_pairs={{0,8},{8,0},{16,24},{24,16},{32,40},{40,32},{48,56},{56,48},{64,72... | collective-permute-start | bytes 2555912 | tf_op jit(solution)/shard_map/ppermute | solution.py:310
  136.7 7.5 %collective-permute-start.16 = (bf16[128,1664]{1,0:T(8,128)(2,1)S(1)}, bf16[128,1664]{1,0:T(8,128)(2,1)}, u32[]{:S(2)}, u32[]{:S(2)}) collective-permute-start(bf16[128,1664]{1,0:T(8,128)(2,1)S(1)} %constant_dynamic-slice_fusion), channel_id=1, source_target_pairs={{0,64},{16,80},{32,96},{48,112},{64,128},{80,144},{96,160},{112,17... | collective-permute-start | bytes 1277960 | tf_op jit(solution)/shard_map/ppermute | solution.py:309
  138.8 16.4 %collective-permute-start.21 = (bf16[208,1664]{1,0:T(8,128)(2,1)}, bf16[208,1664]{1,0:T(8,128)(2,1)}, u32[]{:S(2)}, u32[]{:S(2)}) collective-permute-start(bf16[208,1664]{1,0:T(8,128)(2,1)} %slice.18), channel_id=1, source_target_pairs={{0,2},{1,3},{2,4},{3,5},{4,6},{5,7},{6,0},{7,1},{8,10},{9,11},{10,... | collective-permute-start | bytes 2076680 | tf_op jit(solution)/shard_map/ppermute | solution.py:274
  140.0 15.2 %collective-permute-start.22 = (bf16[208,1664]{1,0:T(8,128)(2,1)S(1)}, bf16[208,1664]{1,0:T(8,128)(2,1)S(1)}, u32[]{:S(2)}, u32[]{:S(2)}) collective-permute-start(bf16[208,1664]{1,0:T(8,128)(2,1)S(1)} %slice.19), channel_id=1, source_target_pairs={{0,6},{1,7},{2,0},{3,1},{4,2},{5,3},{6,4},{7,5},{8,14},{9,15},{10,... | collective-permute-start | bytes 2076680 | tf_op jit(solution)/shard_map/ppermute | solution.py:274
  144.1 27.9 %collective-permute-start.17 = (bf16[128,1664]{1,0:T(8,128)(2,1)}, bf16[128,1664]{1,0:T(8,128)(2,1)S(1)}, u32[]{:S(2)}, u32[]{:S(2)}) collective-permute-start(bf16[128,1664]{1,0:T(8,128)(2,1)} %collective-permute-done.16.first_ref), channel_id=1, source_target_pairs={{0,8},{8,0},{16,24},{24,16},{32,40},{40,32},{48,56},{56,48},{64,72... | collective-permute-start | bytes 1277960 | tf_op jit(solution)/shard_map/ppermute | solution.py:311
  (9 other events, 136.4 us)
where the time goes:
time: 183 us; the launch traced here: 180 us
  waiting for transfers between devices  84.7 us (46%)
  Pallas kernels  42.8 us (23%)
  starting transfers between devices  37.3 us (20%)
  local copies, waits for them, and re-layouts  7.32 us (4%)
  other arithmetic  7.01 us (4%)
    ppermute x1, waiting for transfers between devices, per_device(): shared = lax.ppermute(own, 'col', share)  56.5 us
    pallas_call x3, Pallas kernels, finish(): pl.pallas_call(kernel, grid_spec=pltpu.PrefetchScalarGridSpec(num_scalar_...  22.7 us
    pallas_call x1, Pallas kernels, prune(): pl.pallas_call(prune_kernel, in_specs=[smem, smem, vmem] + [vmem] * LANES...  15.4 us
    ppermute x1, waiting for transfers between devices, per_device(): near = lax.ppermute(own, 'col', ring)  11.9 us
    ppermute x1, starting transfers between devices, per_device(): near_other = lax.ppermute(near, 'col', swap)  11.6 us
    ppermute x1, waiting for transfers between devices, per_device(): lax.ppermute(factor_low, 'row', [(k, k ^ 1) for k in range(LANES)])  7.82 us
    ppermute x7, starting transfers between devices, hop(): return lax.ppermute(array, ('col', 'row'), pairs)  7.6 us
    ppermute x4, waiting for transfers between devices, along(): lax.ppermute(array, 'row', [(row_at(y, zl), row_at(y + dy, zl)) for y in...  7.04 us
  transfers between devices with their start and end apart: 24, of which 5 were waited for; matrix products, arithmetic and copies ran while one was open for 6% of the time, Pallas kernels for 9%

commit v1 on v0

--- a/solution.py
+++ b/solution.py
@@ -161,7 +161,7 @@
 def prune(keep_mask, order, weight, pieces):
     vmem = pl.BlockSpec(memory_space=pltpu.VMEM)
     smem = pl.BlockSpec(memory_space=pltpu.SMEM)
-    quarter = jax.ShapeDtypeStruct((QUARTER, PCOLS), BF)
+    quarter = pltpu.VMEM((QUARTER, PCOLS), BF)
     return pl.pallas_call(
         prune_kernel,
         in_specs=[smem, smem, vmem] + [vmem] * LANES,
@@ -171,6 +171,7 @@
             pltpu.VMEM((PCOLS, PCOLS + 2 * BLK), BF),
             pltpu.VMEM((ROWS_DEV, PCOLS), BF),
         ],
+        compiler_params=pltpu.CompilerParams(vmem_limit_bytes=36 * 2**20),
         name="prune",
     )(keep_mask, order, weight, *pieces)
 
@@ -181,7 +182,7 @@
     return jnp.where(owner > 0, kept_ref[...], trailing)
 
 
-def own_kernel(at_ref, piece_ref, *rest):
+def own_kernel(at_ref, piece_ref, token_ref, *rest):
     parts = rest[:5]
     weight_ref, kept_ref, out_ref, factor_ref = rest[5:]
     for place, part in enumerate(parts):
@@ -222,6 +223,7 @@
         ),
         out_shape=out_shape,
         input_output_aliases={len(inputs) + 2: 0},
+        compiler_params=pltpu.CompilerParams(vmem_limit_bytes=36 * 2**20),
     )(at, *inputs, weight, kept)
 
 
@@ -273,6 +275,7 @@
     def along(array, dy):
         return lax.ppermute(array, "row", [(row_at(y, zl), row_at(y + dy, zl)) for y in range(4) for zl in (0, 1)])
 
+    token = lax.ppermute(factor_low[:16, :BLK], "col", [(0, 1)])
     partner = lax.ppermute(factor_low, "row", [(k, k ^ 1) for k in range(LANES)])
     even = zl_at == 0
     pair = jnp.concatenate(
@@ -314,8 +317,10 @@
         return jnp.stack(values).astype(jnp.int32)
 
     owner = section == 0
-    factor_shape = jax.ShapeDtypeStruct((PCOLS, PCOLS), BF)
-    out, factor_all = finish(own_kernel, 1, ints(x_at, owner, *part_rows), (own, *parts), weight, kept, factor_shape)
+    factor_shape = pltpu.VMEM((PCOLS, PCOLS), BF)
+    out, factor_all = finish(
+        own_kernel, 1, ints(x_at, owner, *part_rows), (own, token, *parts), weight, kept, factor_shape
+    )
     ways = ints((x_at + 3 - 2 * core_at) % 4, (x_at + 1 + 2 * core_at) % 4, owner)
     (out,) = finish(near_kernel, 2, ways, (near, near_other, factor_all), weight, out)
     (out,) = finish(

time: 183 us -> 183 us (level)
  Pallas kernels: 42.8 us -> 36.2 us
  local copies, waits for them, and re-layouts: 7.32 us -> 11.8 us
  starting transfers between devices: 37.3 us -> 40 us
    pallas_call x3, Pallas kernels: 22.7 us -> 18.5 us  [finish(): pl.pallas_call(kernel, grid_spec=pltpu.PrefetchScalarGridSpec(num_scalar_...]
    unnamed x18 -> x12, local copies, waits for them, and re-layouts: 2.81 us -> 5.82 us
    pallas_call x1, Pallas kernels: 15.4 us -> 13.1 us  [prune(): pl.pallas_call(prune_kernel, in_specs=[smem, smem, vmem] + [vmem] * LANES...]
    ppermute x1, waiting for transfers between devices: 7.82 us -> 5.8 us  [per_device(): lax.ppermute(factor_low, 'row', [(k, k ^ 1) for k in range(LANES)])]
  transfers between devices with their start and end apart: 24 -> 25, of which waited for: 5 -> 7; matrix products, arithmetic and copies ran while one was open for 6% -> 6% of each run, Pallas kernels for 9% -> 8%
where the time goes in v1:
time: 183 us; the launch traced here: 180 us
  waiting for transfers between devices  85.3 us (47%)
  starting transfers between devices  40 us (22%)
  Pallas kernels  36.2 us (20%)
  local copies, waits for them, and re-layouts  11.8 us (6%)
  other arithmetic  6.7 us (4%)
    ppermute x1, waiting for transfers between devices, per_device(): shared = lax.ppermute(own, 'col', share)  57.5 us
    pallas_call x3, Pallas kernels, finish(): pl.pallas_call(kernel, grid_spec=pltpu.PrefetchScalarGridSpec(num_scalar_...  18.5 us
    pallas_call x1, Pallas kernels, prune(): pl.pallas_call(prune_kernel, in_specs=[smem, smem, vmem] + [vmem] * LANES...  13.1 us
    ppermute x1, waiting for transfers between devices, per_device(): near = lax.ppermute(own, 'col', ring)  12.8 us
    ppermute x1, starting transfers between devices, per_device(): near_other = lax.ppermute(near, 'col', swap)  12.4 us
    ppermute x7, starting transfers between devices, hop(): return lax.ppermute(array, ('col', 'row'), pairs)  7.51 us
    ppermute x4, waiting for transfers between devices, along(): lax.ppermute(array, 'row', [(row_at(y, zl), row_at(y + dy, zl)) for y in...  7.32 us
    unnamed x12, local copies, waits for them, and re-layouts  5.82 us
  transfers between devices with their start and end apart: 25, of which 7 were waited for; matrix products, arithmetic and copies ran while one was open for 6% of the time, Pallas kernels for 8%

profile of v1, /device:TPU:1, one launch (start us, length us, event | category | flops | bytes accessed | tf_op | source)
XLA Modules:
  0.0 180.2 jit_solution(2074017168138736425)
XLA Ops:
  0.0 4.7 %local_part.1 = (bf16[208,1920]{1,0:T(8,128)(2,1)}, bf16[208,1664]{1,0:T(8,128)(2,1)}) custom-call(s32[1]{0:T(128)} %bitcast.4.lane_ref, f32[208,1664]{1,0:T(8,128)} %factor_ref.1), custom_call_target="tpu_custom_call" | custom-call | tf_op jit(solution)/shard_map/local_part/pallas_call | solution.py:90
  7.6 1.6 collective-permute-start.4
  9.1 1.5 collective-permute-start.5
  10.7 1.6 collective-permute-start.6
  13.3 2.0 %copy-done = bf16[1024,1664]{1,0:T(8,128)(2,1)S(1)} copy-done((bf16[1024,1664]{1,0:T(8,128)(2,1)S(1)}, bf16[1024,1664]{1,0:T(8,128)(2,1)}, u32[]{:S(2)}) %copy-start) | copy-done | bytes 3407896
  18.2 13.1 %prune.1 = (bf16[256,1664]{1,0:T(8,128)(2,1)S(1)}, bf16[256,1664]{1,0:T(8,128)(2,1)}, bf16[256,1664]{1,0:T(8,128)(2,1)}, bf16[256,1664]{1,0:T(8,128)(2,1)}, bf16[1024,1664]{1,0:T(8,128)(2,1)}) custom-call(s32[8,13]{1,0:T(8,128)S(1)} %copy-done.5, s32[8]{0:T(128)S(1)} %stack.91.order_ref, bf16[1024,1664]{1,0:T(8,128)(2,1)S(1)} %copy-done, ...), custom_call_target="tpu_custom_call" | custom-call | tf_op jit(solution)/shard_map/prune/pallas_call | solution.py:165
  32.7 1.6 collective-permute-start.9
  38.6 1.4 collective-permute-start.13
  40.0 2.4 %collective-permute-start.19 = (bf16[208,1664]{1,0:T(8,128)(2,1)}, bf16[208,1664]{1,0:T(8,128)(2,1)}, u32[]{:S(2)}, u32[]{:S(2)}) collective-permute-start(bf16[208,1664]{1,0:T(8,128)(2,1)} %get-tuple-element.19), channel_id=1, source_target_pairs={{0,1},{1,0},{2,3},{3,2},{4,5},{5,4},{6,7},{7,6},{8,9},{9,8},{10,11... | collective-permute-start | bytes 2076680 | tf_op jit(solution)/shard_map/ppermute | solution.py:279
  42.5 1.6 fusion
  45.3 5.8 %collective-permute-done.19 = bf16[208,1664]{1,0:T(8,128)(2,1)} collective-permute-done((bf16[208,1664]{1,0:T(8,128)(2,1)}, bf16[208,1664]{1,0:T(8,128)(2,1)}, u32[]{:S(2)}, u32[]{:S(2)}) %collective-permute-start.19) | collective-permute-done | bytes 692256 | tf_op jit(solution)/shard_map/ppermute | solution.py:279
  55.1 1.4 collective-permute-start.21
  56.5 57.5 %collective-permute-done.14 = bf16[256,1664]{1,0:T(8,128)(2,1)S(1)} collective-permute-done((bf16[256,1664]{1,0:T(8,128)(2,1)S(1)}, bf16[256,1664]{1,0:T(8,128)(2,1)S(1)}, u32[]{:S(2)}, u32[]{:S(2)}) %collective-permute-start.14) | collective-permute-done | bytes 852000 | tf_op jit(solution)/shard_map/ppermute | solution.py:309
  115.0 12.8 %collective-permute-done.15.first_ref = bf16[256,1664]{1,0:T(8,128)(2,1)} collective-permute-done((bf16[256,1664]{1,0:T(8,128)(2,1)}, bf16[256,1664]{1,0:T(8,128)(2,1)}, u32[]{:S(2)}, u32[]{:S(2)}) %collective-permute-start.15) | collective-permute-done | bytes 852000 | tf_op jit(solution)/shard_map/ppermute | solution.py:311
  127.8 12.4 %collective-permute-start.24 = (bf16[256,1664]{1,0:T(8,128)(2,1)}, bf16[256,1664]{1,0:T(8,128)(2,1)}, u32[]{:S(2)}, u32[]{:S(2)}) collective-permute-start(bf16[256,1664]{1,0:T(8,128)(2,1)} %collective-permute-done.15.first_ref), channel_id=1, source_target_pairs={{0,8},{8,0},{16,24},{24,16},{32,40},{40,32},{48,56},{56,48},{64,72... | collective-permute-start | bytes 2555912 | tf_op jit(solution)/shard_map/ppermute | solution.py:313
  141.3 2.0 %slice.22 = bf16[208,1664]{1,0:T(8,128)(2,1)} slice(bf16[416,1664]{1,0:T(8,128)(2,1)} %collective-permute-done.20.rest_1_), slice={[0:208], [0:1664]} | slice | bytes 1384448 | tf_op jit(solution)/shard_map/slice | solution.py:286
  143.3 2.0 %slice.23 = bf16[208,1664]{1,0:T(8,128)(2,1)} slice(bf16[416,1664]{1,0:T(8,128)(2,1)} %collective-permute-done.21.rest_2_), slice={[208:416], [0:1664]} | slice | bytes 1384448 | tf_op jit(solution)/shard_map/slice | solution.py:287
  145.3 2.7 %collective-permute-start.23 = (bf16[208,1664]{1,0:T(8,128)(2,1)}, bf16[208,1664]{1,0:T(8,128)(2,1)}, u32[]{:S(2)}, u32[]{:S(2)}) collective-permute-start(bf16[208,1664]{1,0:T(8,128)(2,1)} %slice.23), channel_id=1, source_target_pairs={{0,6},{1,7},{2,0},{3,1},{4,2},{5,3},{6,4},{7,5},{8,14},{9,15},{10,... | collective-permute-start | bytes 2076680 | tf_op jit(solution)/shard_map/ppermute | solution.py:276
  148.6 2.1 %collective-permute-start.17 = (bf16[128,1664]{1,0:T(8,128)(2,1)}, bf16[128,1664]{1,0:T(8,128)(2,1)}, u32[]{:S(2)}, u32[]{:S(2)}) collective-permute-start(bf16[128,1664]{1,0:T(8,128)(2,1)} %collective-permute-done.16.first_ref), channel_id=1, source_target_pairs={{0,8},{8,0},{16,24},{24,16},{32,40},{40,32},{48,56},{56,48},{64,72... | collective-permute-start | bytes 1277960 | tf_op jit(solution)/shard_map/ppermute | solution.py:314
  151.4 1.5 collective-permute-start.18
  154.4 6.3 %collective-permute-done.22.rest_3_ = bf16[208,1664]{1,0:T(8,128)(2,1)} collective-permute-done((bf16[208,1664]{1,0:T(8,128)(2,1)}, bf16[208,1664]{1,0:T(8,128)(2,1)}, u32[]{:S(2)}, u32[]{:S(2)}) %collective-permute-start.22) | collective-permute-done | bytes 692256 | tf_op jit(solution)/shard_map/ppermute | solution.py:276
  161.8 6.7 %shard_map.37 = (bf16[1024,1664]{1,0:T(8,128)(2,1)}, bf16[1664,1664]{1,0:T(8,128)(2,1)S(1)}) custom-call(s32[7]{0:T(128)S(1)} %stack.98.at_ref, bf16[256,1664]{1,0:T(8,128)(2,1)} %broadcast_select_fusion.piece_ref, bf16[16,128]{1,0:T(8,128)(2,1)S(1)} %collective-permute-done.18.token_ref, ...), custom_call_target="tpu_custom_call", output_to_operand_aliasing={{0}: (9, {})} | custom-call | tf_op jit(solution)/shard_map/pallas_call | solution.py:215
  168.5 6.9 %shard_map.38.kept_ref = bf16[1024,1664]{1,0:T(8,128)(2,1)} custom-call(s32[3]{0:T(128)S(1)} %pad_add_fusion.1.at_ref, bf16[256,1664]{1,0:T(8,128)(2,1)} %collective-permute-done.15.first_ref, bf16[256,1664]{1,0:T(8,128)(2,1)} %collective-permute-done.24.second_ref, ...), custom_call_target="tpu_custom_call", output_to_operand_aliasing={{}: (5, {})} | custom-call | tf_op jit(solution)/shard_map/pallas_call | solution.py:215
  175.4 4.8 %shard_map.39 = bf16[1024,1664]{1,0:T(8,128)(2,1)} custom-call(s32[4]{0:T(128)S(1)} %pad_add_fusion.at_ref, bf16[128,1664]{1,0:T(8,128)(2,1)} %collective-permute-done.16.first_ref, bf16[128,1664]{1,0:T(8,128)(2,1)} %collective-permute-done.17.second_ref, bf16[1664,1664]{1,0:T(8,128)(2,1)S(1)} %get-tuple-element.21.factor_ref, ...), custom_call_target="tpu_custom_call", output_to_operand_aliasing={{}: (5, {})} | custom-call | tf_op jit(solution)/shard_map/pallas_call | solution.py:215
  (58 shorter events, 23.7 us)
Async XLA Ops:
  4.7 4.4 %collective-permute-start = (bf16[208,1920]{1,0:T(8,128)(2,1)}, bf16[208,1920]{1,0:T(8,128)(2,1)S(1)}, u32[]{:S(2)}, u32[]{:S(2)}) collective-permute-start(bf16[208,1920]{1,0:T(8,128)(2,1)} %get-tuple-element.14.rest_0_), channel_id=1, source_target_pairs={{0,2},{1,3},{2,4},{3,5},{4,6},{5,7},{6,0},{7,1}} | collective-permute-start | bytes 2396168 | tf_op jit(solution)/shard_map/ppermute | solution.py:252
  5.4 5.3 %collective-permute-start.1 = (bf16[208,1920]{1,0:T(8,128)(2,1)}, bf16[208,1920]{1,0:T(8,128)(2,1)S(1)}, u32[]{:S(2)}, u32[]{:S(2)}) collective-permute-start(bf16[208,1920]{1,0:T(8,128)(2,1)} %get-tuple-element.14.rest_0_), channel_id=1, source_target_pairs={{0,7},{1,6},{2,1},{3,0},{4,3},{5,2},{6,5},{7,4}} | collective-permute-start | bytes 2396168 | tf_op jit(solution)/shard_map/ppermute | solution.py:252
  6.1 6.2 %collective-permute-start.2 = (bf16[208,1920]{1,0:T(8,128)(2,1)}, bf16[208,1920]{1,0:T(8,128)(2,1)S(1)}, u32[]{:S(2)}, u32[]{:S(2)}) collective-permute-start(bf16[208,1920]{1,0:T(8,128)(2,1)} %get-tuple-element.14.rest_0_), channel_id=1, source_target_pairs={{0,3},{1,2},{2,5},{3,4},{4,7},{5,6},{6,1},{7,0}} | collective-permute-start | bytes 2396168 | tf_op jit(solution)/shard_map/ppermute | solution.py:252
  6.8 5.5 %collective-permute-start.3 = (bf16[208,1920]{1,0:T(8,128)(2,1)}, bf16[208,1920]{1,0:T(8,128)(2,1)S(1)}, u32[]{:S(2)}, u32[]{:S(2)}) collective-permute-start(bf16[208,1920]{1,0:T(8,128)(2,1)} %get-tuple-element.14.rest_0_), channel_id=1, source_target_pairs={{0,6},{1,7},{2,0},{3,1},{4,2},{5,3},{6,4},{7,5}} | collective-permute-start | bytes 2396168 | tf_op jit(solution)/shard_map/ppermute | solution.py:252
  7.6 5.7 %collective-permute-start.4 = (bf16[208,1920]{1,0:T(8,128)(2,1)}, bf16[208,1920]{1,0:T(8,128)(2,1)}, u32[]{:S(2)}, u32[]{:S(2)}) collective-permute-start(bf16[208,1920]{1,0:T(8,128)(2,1)} %get-tuple-element.14.rest_0_), channel_id=1, source_target_pairs={{0,1},{1,0},{2,3},{3,2},{4,5},{5,4},{6,7},{7,6}} | collective-permute-start | bytes 2396168 | tf_op jit(solution)/shard_map/ppermute | solution.py:252
  9.1 4.1 %collective-permute-start.5 = (bf16[208,1920]{1,0:T(8,128)(2,1)S(1)}, bf16[208,1920]{1,0:T(8,128)(2,1)}, u32[]{:S(2)}, u32[]{:S(2)}) collective-permute-start(bf16[208,1920]{1,0:T(8,128)(2,1)S(1)} %collective-permute-done.rest_1_), channel_id=1, source_target_pairs={{0,2},{1,3},{2,4},{3,5},{4,6},{5,7},{6,0},{7,1}} | collective-permute-start | bytes 2396168 | tf_op jit(solution)/shard_map/ppermute | solution.py:252
  10.7 2.6 %collective-permute-start.6 = (bf16[208,1920]{1,0:T(8,128)(2,1)S(1)}, bf16[208,1920]{1,0:T(8,128)(2,1)}, u32[]{:S(2)}, u32[]{:S(2)}) collective-permute-start(bf16[208,1920]{1,0:T(8,128)(2,1)S(1)} %collective-permute-done.1.rest_2_), channel_id=1, source_target_pairs={{0,6},{1,7},{2,0},{3,1},{4,2},{5,3},{6,4},{7,5}} | collective-permute-start | bytes 2396168 | tf_op jit(solution)/shard_map/ppermute | solution.py:252
  31.3 3.0 %collective-permute-start.7 = (bf16[256,1664]{1,0:T(8,128)(2,1)}, bf16[256,1664]{1,0:T(8,128)(2,1)S(1)}, u32[]{:S(2)}, u32[]{:S(2)}) collective-permute-start(bf16[256,1664]{1,0:T(8,128)(2,1)} %get-tuple-element.16), channel_id=1, source_target_pairs={{0,128},{1,129},{2,130},{3,131},{4,132},{5,133},{6,134},{7,135}} | collective-permute-start | bytes 2555912 | tf_op jit(solution)/shard_map/ppermute | solution.py:295
  32.0 2.3 %collective-permute-start.8 = (bf16[256,1664]{1,0:T(8,128)(2,1)}, bf16[256,1664]{1,0:T(8,128)(2,1)S(1)}, u32[]{:S(2)}, u32[]{:S(2)}) collective-permute-start(bf16[256,1664]{1,0:T(8,128)(2,1)} %get-tuple-element.17), channel_id=1, source_target_pairs={{0,64},{1,65},{2,66},{3,67},{4,68},{5,69},{6,70},{7,71}} | collective-permute-start | bytes 2555912 | tf_op jit(solution)/shard_map/ppermute | solution.py:295
  32.7 1.6 collective-permute-start.9
  36.3 2.2 %collective-permute-start.11 = (bf16[256,1664]{1,0:T(8,128)(2,1)S(1)}, bf16[256,1664]{1,0:T(8,128)(2,1)S(1)}, u32[]{:S(2)}, u32[]{:S(2)}) collective-permute-start(bf16[256,1664]{1,0:T(8,128)(2,1)S(1)} %add_select_fusion), channel_id=1, source_target_pairs={{0,48},{64,112},{128,176},{192,240},{1,49},{65,113},{129,177},{193... | collective-permute-start | bytes 2555912 | tf_op jit(solution)/shard_map/ppermute | solution.py:299
  37.1 5.4 %collective-permute-start.12 = (bf16[128,1664]{1,0:T(8,128)(2,1)S(1)}, bf16[128,1664]{1,0:T(8,128)(2,1)}, u32[]{:S(2)}, u32[]{:S(2)}) collective-permute-start(bf16[128,1664]{1,0:T(8,128)(2,1)S(1)} %slice.20), channel_id=1, source_target_pairs={{16,32},{80,96},{144,160},{208,224},{17,33},{81,97},{145,161},{209... | collective-permute-start | bytes 1277960 | tf_op jit(solution)/shard_map/ppermute | solution.py:300
  38.6 3.9 %collective-permute-start.13 = (bf16[128,1664]{1,0:T(8,128)(2,1)S(1)}, bf16[128,1664]{1,0:T(8,128)(2,1)}, u32[]{:S(2)}, u32[]{:S(2)}) collective-permute-start(bf16[128,1664]{1,0:T(8,128)(2,1)S(1)} %slice.21), channel_id=1, source_target_pairs={{48,32},{112,96},{176,160},{240,224},{49,33},{113,97},{177,161},{2... | collective-permute-start | bytes 1277960 | tf_op jit(solution)/shard_map/ppermute | solution.py:301
  40.0 11.1 %collective-permute-start.19 = (bf16[208,1664]{1,0:T(8,128)(2,1)}, bf16[208,1664]{1,0:T(8,128)(2,1)}, u32[]{:S(2)}, u32[]{:S(2)}) collective-permute-start(bf16[208,1664]{1,0:T(8,128)(2,1)} %get-tuple-element.19), channel_id=1, source_target_pairs={{0,1},{1,0},{2,3},{3,2},{4,5},{5,4},{6,7},{7,6},{8,9},{9,8},{10,11... | collective-permute-start | bytes 2076680 | tf_op jit(solution)/shard_map/ppermute | solution.py:279
  44.0 70.0 %collective-permute-start.14 = (bf16[256,1664]{1,0:T(8,128)(2,1)S(1)}, bf16[256,1664]{1,0:T(8,128)(2,1)S(1)}, u32[]{:S(2)}, u32[]{:S(2)}) collective-permute-start(bf16[256,1664]{1,0:T(8,128)(2,1)S(1)} %fusion), channel_id=1, source_target_pairs={{0,8},{16,24},{32,40},{48,56},{64,72},{80,88},{96,104},{112,120},{... | collective-permute-start | bytes 2555912 | tf_op jit(solution)/shard_map/ppermute | solution.py:309
  53.8 87.5 %collective-permute-start.20 = (bf16[416,1664]{1,0:T(8,128)(2,1)}, bf16[416,1664]{1,0:T(8,128)(2,1)}, u32[]{:S(2)}, u32[]{:S(2)}) collective-permute-start(bf16[416,1664]{1,0:T(8,128)(2,1)} %pad_maximum_fusion.rest_0_), channel_id=1, source_target_pairs={{0,2},{1,3},{2,4},{3,5},{4,6},{5,7},{6,0},{7,1},{8,10},{9,11},{10,... | collective-permute-start | bytes 4153352 | tf_op jit(solution)/shard_map/ppermute | solution.py:276
  55.1 88.2 %collective-permute-start.21 = (bf16[416,1664]{1,0:T(8,128)(2,1)}, bf16[416,1664]{1,0:T(8,128)(2,1)}, u32[]{:S(2)}, u32[]{:S(2)}) collective-permute-start(bf16[416,1664]{1,0:T(8,128)(2,1)} %pad_maximum_fusion.rest_0_), channel_id=1, source_target_pairs={{0,6},{1,7},{2,0},{3,1},{4,2},{5,3},{6,4},{7,5},{8,14},{9,15},{10,... | collective-permute-start | bytes 4153352 | tf_op jit(solution)/shard_map/ppermute | solution.py:276
  115.0 12.8 %collective-permute-start.15 = (bf16[256,1664]{1,0:T(8,128)(2,1)}, bf16[256,1664]{1,0:T(8,128)(2,1)}, u32[]{:S(2)}, u32[]{:S(2)}) collective-permute-start(bf16[256,1664]{1,0:T(8,128)(2,1)} %broadcast_select_fusion.piece_ref), channel_id=1, source_target_pairs={{0,64},{16,80},{32,96},{48,112},{64,128},{80,144},{96,160},{112,17... | collective-permute-start | bytes 2555912 | tf_op jit(solution)/shard_map/ppermute | solution.py:311
  127.8 40.7 %collective-permute-start.24 = (bf16[256,1664]{1,0:T(8,128)(2,1)}, bf16[256,1664]{1,0:T(8,128)(2,1)}, u32[]{:S(2)}, u32[]{:S(2)}) collective-permute-start(bf16[256,1664]{1,0:T(8,128)(2,1)} %collective-permute-done.15.first_ref), channel_id=1, source_target_pairs={{0,8},{8,0},{16,24},{24,16},{32,40},{40,32},{48,56},{56,48},{64,72... | collective-permute-start | bytes 2555912 | tf_op jit(solution)/shard_map/ppermute | solution.py:313
  141.2 7.5 %collective-permute-start.16 = (bf16[128,1664]{1,0:T(8,128)(2,1)S(1)}, bf16[128,1664]{1,0:T(8,128)(2,1)}, u32[]{:S(2)}, u32[]{:S(2)}) collective-permute-start(bf16[128,1664]{1,0:T(8,128)(2,1)S(1)} %constant_dynamic-slice_fusion), channel_id=1, source_target_pairs={{0,64},{16,80},{32,96},{48,112},{64,128},{80,144},{96,160},{112,17... | collective-permute-start | bytes 1277960 | tf_op jit(solution)/shard_map/ppermute | solution.py:312
  143.3 17.5 %collective-permute-start.22 = (bf16[208,1664]{1,0:T(8,128)(2,1)}, bf16[208,1664]{1,0:T(8,128)(2,1)}, u32[]{:S(2)}, u32[]{:S(2)}) collective-permute-start(bf16[208,1664]{1,0:T(8,128)(2,1)} %slice.22), channel_id=1, source_target_pairs={{0,2},{1,3},{2,4},{3,5},{4,6},{5,7},{6,0},{7,1},{8,10},{9,11},{10,... | collective-permute-start | bytes 2076680 | tf_op jit(solution)/shard_map/ppermute | solution.py:276
  145.3 16.4 %collective-permute-start.23 = (bf16[208,1664]{1,0:T(8,128)(2,1)}, bf16[208,1664]{1,0:T(8,128)(2,1)}, u32[]{:S(2)}, u32[]{:S(2)}) collective-permute-start(bf16[208,1664]{1,0:T(8,128)(2,1)} %slice.23), channel_id=1, source_target_pairs={{0,6},{1,7},{2,0},{3,1},{4,2},{5,3},{6,4},{7,5},{8,14},{9,15},{10,... | collective-permute-start | bytes 2076680 | tf_op jit(solution)/shard_map/ppermute | solution.py:276
  148.6 26.8 %collective-permute-start.17 = (bf16[128,1664]{1,0:T(8,128)(2,1)}, bf16[128,1664]{1,0:T(8,128)(2,1)}, u32[]{:S(2)}, u32[]{:S(2)}) collective-permute-start(bf16[128,1664]{1,0:T(8,128)(2,1)} %collective-permute-done.16.first_ref), channel_id=1, source_target_pairs={{0,8},{8,0},{16,24},{24,16},{32,40},{40,32},{48,56},{56,48},{64,72... | collective-permute-start | bytes 1277960 | tf_op jit(solution)/shard_map/ppermute | solution.py:314
  151.4 3.0 %collective-permute-start.18 = (bf16[16,128]{1,0:T(8,128)(2,1)S(1)}, bf16[16,128]{1,0:T(8,128)(2,1)S(1)}, u32[]{:S(2)}, u32[]{:S(2)}) collective-permute-start(bf16[16,128]{1,0:T(8,128)(2,1)S(1)} %slice.17), channel_id=1, source_target_pairs={{0,8},{1,9},{2,10},{3,11},{4,12},{5,13},{6,14},{7,15}} | collective-permute-start | bytes 12296 | tf_op jit(solution)/shard_map/ppermute | solution.py:278
  (7 other events, 54.0 us)

commit v2 on v0

--- a/solution.py
+++ b/solution.py
@@ -15,7 +15,7 @@
 NBLK = PCOLS // BLK
 ROWS_DEV = 1024
 QUARTER = 256
-HALF = 128
+FORWARD = 64
 BF = jnp.bfloat16
 F32 = jnp.float32
 
@@ -103,13 +103,20 @@
     )(lane, factor)
 
 
-def prune_kernel(keep_ref, order_ref, weight_ref, *rest):
+def prune_kernel(keep_ref, order_ref, weight_hbm, *rest):
     pieces = rest[:LANES]
-    quarter_refs = rest[LANES : LANES + 4]
-    kept_ref, factor_ref, errors_ref = rest[LANES + 4 :]
+    part_refs = rest[LANES : 2 * LANES]
+    kept_ref, factor_ref, errors_ref, weight_ref, sems = rest[2 * LANES :]
+    copies = [pltpu.make_async_copy(weight_hbm, weight_ref, sems.at[LANES])]
     for place in range(LANES):
         start = pl.multiple_of(order_ref[place] * LANE_ROWS, 16)
-        factor_ref[pl.ds(start, LANE_ROWS), :] = pieces[place][...]
+        copies.append(
+            pltpu.make_async_copy(pieces[place], factor_ref.at[pl.ds(start, LANE_ROWS), :], sems.at[place])
+        )
+    for copy in copies:
+        copy.start()
+    for copy in copies:
+        copy.wait()
     row = lax.broadcasted_iota(jnp.int32, (BLK, BLK), 0)
     column = lax.broadcasted_iota(jnp.int32, (BLK, BLK), 1)
     eye = (row == column).astype(F32)
@@ -151,8 +158,7 @@
                 keep = keep_ref[group, at // BLK] > 0
                 error = jnp.where(keep, jnp.zeros((BLK, BLK), BF), solved[top : top + BLK])
                 errors_ref[top : top + BLK, at : at + BLK] = error
-                inner = top % QUARTER
-                quarter_refs[top // QUARTER][inner : inner + BLK, at : at + BLK] = error
+                part_refs[group][:, at : at + BLK] = error
                 kept_ref[top : top + BLK, at : at + BLK] = jnp.where(
                     keep, high[top : top + BLK], jnp.zeros((BLK, BLK), BF)
                 )
@@ -161,15 +167,18 @@
 def prune(keep_mask, order, weight, pieces):
     vmem = pl.BlockSpec(memory_space=pltpu.VMEM)
     smem = pl.BlockSpec(memory_space=pltpu.SMEM)
-    quarter = jax.ShapeDtypeStruct((QUARTER, PCOLS), BF)
+    hbm = pl.BlockSpec(memory_space=pl.ANY)
+    part = jax.ShapeDtypeStruct((BLK, PCOLS), BF)
     return pl.pallas_call(
         prune_kernel,
-        in_specs=[smem, smem, vmem] + [vmem] * LANES,
-        out_specs=(vmem,) * 5,
-        out_shape=(quarter,) * 4 + (jax.ShapeDtypeStruct((ROWS_DEV, PCOLS), BF),),
+        in_specs=[smem, smem, hbm] + [hbm] * LANES,
+        out_specs=(vmem,) * (LANES + 1),
+        out_shape=(part,) * LANES + (jax.ShapeDtypeStruct((ROWS_DEV, PCOLS), BF),),
         scratch_shapes=[
             pltpu.VMEM((PCOLS, PCOLS + 2 * BLK), BF),
             pltpu.VMEM((ROWS_DEV, PCOLS), BF),
+            pltpu.VMEM((ROWS_DEV, PCOLS), BF),
+            pltpu.SemaphoreType.DMA((LANES + 1,)),
         ],
         name="prune",
     )(keep_mask, order, weight, *pieces)
@@ -181,27 +190,33 @@
     return jnp.where(owner > 0, kept_ref[...], trailing)
 
 
-def own_kernel(at_ref, piece_ref, *rest):
+def own_kernel(at_ref, first_ref, second_ref, token_ref, *rest):
     parts = rest[:5]
     weight_ref, kept_ref, out_ref, factor_ref = rest[5:]
     for place, part in enumerate(parts):
         start = pl.multiple_of(at_ref[2 + place] * LANE_ROWS, 16)
         factor_ref[pl.ds(start, part.shape[0]), :] = part[...]
-    out_ref[...] = subtract(piece_ref[...], factor_ref[...], weight_ref, kept_ref, at_ref[1])
-
-
-def near_kernel(at_ref, first_ref, second_ref, factor_ref, weight_ref, kept_ref, out_ref):
-    for step, piece_ref in enumerate((first_ref, second_ref)):
+    piece = jnp.concatenate([first_ref[...], second_ref[...]], axis=0)
+    out_ref[...] = subtract(piece, factor_ref[...], weight_ref, kept_ref, at_ref[1])
+
+
+def near_kernel(at_ref, *rest):
+    pieces = rest[:4]
+    factor_ref, weight_ref, kept_ref, out_ref = rest[4:]
+    for step in range(2):
 
         @pl.when(pl.program_id(0) == step)
         def _():
-            out_ref[...] = subtract(piece_ref[...], factor_ref[...], weight_ref, kept_ref, at_ref[2])
-
-
-def far_kernel(at_ref, first_ref, second_ref, factor_ref, weight_ref, kept_ref, out_ref, piece_ref):
-    for place, half_ref in enumerate((first_ref, second_ref)):
-        start = pl.multiple_of(at_ref[2 + place] * HALF, HALF)
-        piece_ref[pl.ds(start, HALF), :] = half_ref[...]
+            piece = jnp.concatenate([pieces[2 * step][...], pieces[2 * step + 1][...]], axis=0)
+            out_ref[...] = subtract(piece, factor_ref[...], weight_ref, kept_ref, at_ref[2])
+
+
+def far_kernel(at_ref, *rest):
+    pieces = rest[:4]
+    factor_ref, weight_ref, kept_ref, out_ref, piece_ref = rest[4:]
+    for place, part_ref in enumerate(pieces):
+        start = pl.multiple_of(at_ref[2 + place] * FORWARD, FORWARD)
+        piece_ref[pl.ds(start, FORWARD), :] = part_ref[...]
     out_ref[...] = subtract(piece_ref[...], factor_ref[...], weight_ref, kept_ref, at_ref[1])
 
 
@@ -268,11 +283,12 @@
         row_at(y_at + 2, zl_at),
         row_at(y_at + 2, 1 - zl_at),
     ]
-    *quarters, kept = prune(keep_mask, jnp.stack(order).astype(jnp.int32), weight, pieces)
+    *parts_out, kept = prune(keep_mask, jnp.stack(order).astype(jnp.int32), weight, pieces)
 
     def along(array, dy):
         return lax.ppermute(array, "row", [(row_at(y, zl), row_at(y + dy, zl)) for y in range(4) for zl in (0, 1)])
 
+    token = lax.ppermute(factor_low[:16, :BLK], "col", [(0, 1)])
     partner = lax.ppermute(factor_low, "row", [(k, k ^ 1) for k in range(LANES)])
     even = zl_at == 0
     pair = jnp.concatenate(
@@ -287,42 +303,50 @@
         row_at(y_at, 0), row_at(y_at + 3, 0), row_at(y_at + 1, 0), row_at(y_at + 2, 0), row_at(y_at + 2, 1)
     ]
 
-    got = None
-    for k in (2, 1, 3):
-        sent = lax.ppermute(quarters[k], "col", [(0, col_at(k, 0, 0))])
-        got = sent if got is None else got + sent
-    own = jnp.where(x_at == 0, quarters[0], got)
-    up = lax.ppermute(own, "col", [(col_at(x, 0, 0), col_at(x, 1, 0)) for x in range(4)])
-    down = lax.ppermute(own, "col", [(col_at(x, 0, 0), col_at(x, 3, 0)) for x in range(4)])
-    far_a = lax.ppermute(up[:HALF], "col", [(col_at(x, 1, 0), col_at(x, 2, 0)) for x in range(4)])
-    far_b = lax.ppermute(down[HALF:], "col", [(col_at(x, 3, 0), col_at(x, 2, 0)) for x in range(4)])
-    own = jnp.where(zh_at == 0, own, up + down + jnp.concatenate([far_a, far_b], axis=0))
-
     places = [(x, z) for x in range(4) for z in range(4)]
     share = [(col_at(x, z, 0), col_at(x, z, 1)) for x, z in places]
     swap = [(col_at(x, z, c), col_at(x, z, 1 - c)) for x, z in places for c in (0, 1)]
     ring = [(col_at(x, z, 0), col_at(x + 1, z, 0)) for x, z in places]
     ring += [(col_at(x, z, 1), col_at(x - 1, z, 1)) for x, z in places]
-    shared = lax.ppermute(own, "col", share)
-    own = jnp.where(core_at == 0, own, shared)
-    near = lax.ppermute(own, "col", ring)
-    far = lax.ppermute(lax.dynamic_slice(near, (core_at * HALF, 0), (HALF, PCOLS)), "col", ring)
-    near_other = lax.ppermute(near, "col", swap)
-    far_other = lax.ppermute(far, "col", swap)
+    owns, nears, near_others, fars, far_others = [], [], [], [], []
+    for chunk in (0, 1):
+        got = None
+        for k in (2, 1, 3):
+            sent = lax.ppermute(parts_out[2 * k + chunk], "col", [(0, col_at(k, 0, 0))])
+            got = sent if got is None else got + sent
+        own = jnp.where(x_at == 0, parts_out[chunk], got)
+        up = lax.ppermute(own, "col", [(col_at(x, 0, 0), col_at(x, 1, 0)) for x in range(4)])
+        down = lax.ppermute(own, "col", [(col_at(x, 0, 0), col_at(x, 3, 0)) for x in range(4)])
+        far_a = lax.ppermute(up[:FORWARD], "col", [(col_at(x, 1, 0), col_at(x, 2, 0)) for x in range(4)])
+        far_b = lax.ppermute(down[FORWARD:], "col", [(col_at(x, 3, 0), col_at(x, 2, 0)) for x in range(4)])
+        own = jnp.where(zh_at == 0, own, up + down + jnp.concatenate([far_a, far_b], axis=0))
+
+        shared = lax.ppermute(own, "col", share)
+        own = jnp.where(core_at == 0, own, shared)
+        near = lax.ppermute(own, "col", ring)
+        onward = lax.dynamic_slice(near, (core_at * FORWARD, 0), (FORWARD, PCOLS))
+        far = lax.ppermute(onward, "col", ring)
+        owns.append(own)
+        nears.append(near)
+        fars.append(far)
+        near_others.append(lax.ppermute(near, "col", swap))
+        far_others.append(lax.ppermute(far, "col", swap))
 
     def ints(*values):
-        return jnp.stack(values).astype(jnp.int32)
+        return jnp.stack([jnp.asarray(value) for value in values]).astype(jnp.int32)
 
     owner = section == 0
     factor_shape = jax.ShapeDtypeStruct((PCOLS, PCOLS), BF)
-    out, factor_all = finish(own_kernel, 1, ints(x_at, owner, *part_rows), (own, *parts), weight, kept, factor_shape)
+    out, factor_all = finish(
+        own_kernel, 1, ints(x_at, owner, *part_rows), (*owns, token, *parts), weight, kept, factor_shape
+    )
     ways = ints((x_at + 3 - 2 * core_at) % 4, (x_at + 1 + 2 * core_at) % 4, owner)
-    (out,) = finish(near_kernel, 2, ways, (near, near_other, factor_all), weight, out)
+    (out,) = finish(near_kernel, 2, ways, (*nears, *near_others, factor_all), weight, out)
     (out,) = finish(
         far_kernel,
         1,
-        ints((x_at + 2) % 4, owner, core_at, 1 - core_at),
-        (far, far_other, factor_all),
+        ints((x_at + 2) % 4, owner, core_at, 2 + core_at, 1 - core_at, 3 - core_at),
+        (*fars, *far_others, factor_all),
         weight,
         out,
         scratch=[pltpu.VMEM((QUARTER, PCOLS), BF)],

time: 183 us -> 169 us (0.923)
  waiting for transfers between devices: 84.7 us -> 59.2 us
  starting transfers between devices: 37.3 us -> 50.7 us
  other arithmetic: 7.01 us -> 4.42 us
    ppermute x1 -> x2, waiting for transfers between devices: 11.9 us -> 0.01 us  [per_device(): near = lax.ppermute(own, 'col', ring)]
    ppermute x8 -> x17, starting transfers between devices: 18.8 us -> 27.3 us  [the longest x2 8.92 us: per_device(): near_others.append(lax.ppermute(near, 'col', swap))]
    ppermute x1 -> x2, waiting for transfers between devices: 56.5 us -> 49 us  [per_device(): shared = lax.ppermute(own, 'col', share)]
    ppermute x4, waiting for transfers between devices: 7.04 us -> 0.01 us  [along(): lax.ppermute(array, 'row', [(row_at(y, zl), row_at(y + dy, zl)) for y in...]
    ppermute x1 -> x2, starting transfers between devices: 0.08 us -> 2.59 us  [per_device(): near = lax.ppermute(own, 'col', ring)]
    dynamic_slice x1 -> x2, local copies, waits for them, and re-layouts: 0.03 us -> 1.9 us  [per_device(): onward = lax.dynamic_slice(near, (core_at * FORWARD, 0), (FORWARD, PCOLS))]
  transfers between devices with their start and end apart: 24 -> 37, of which waited for: 5 -> 4; matrix products, arithmetic and copies ran while one was open for 6% -> 7% of each run, Pallas kernels for 9% -> 10%
where the time goes in v2:
time: 169 us; the launch traced here: 167 us
  waiting for transfers between devices  59.2 us (35%)
  starting transfers between devices  50.7 us (30%)
  Pallas kernels  43.4 us (26%)
  local copies, waits for them, and re-layouts  8.6 us (5%)
  other arithmetic  4.42 us (3%)
    ppermute x2, waiting for transfers between devices, per_device(): shared = lax.ppermute(own, 'col', share)  49 us
    pallas_call x3, Pallas kernels, finish(): pl.pallas_call(kernel, grid_spec=pltpu.PrefetchScalarGridSpec(num_scalar_...  22.8 us
    pallas_call x1, Pallas kernels, prune(): pl.pallas_call(prune_kernel, in_specs=[smem, smem, hbm] + [hbm] * LANES,...  15.8 us
    ppermute x1, waiting for transfers between devices, per_device(): lax.ppermute(factor_low, 'row', [(k, k ^ 1) for k in range(LANES)])  9.06 us
    ppermute x2, starting transfers between devices, per_device(): near_others.append(lax.ppermute(near, 'col', swap))  8.92 us
    ppermute x7, starting transfers between devices, hop(): return lax.ppermute(array, ('col', 'row'), pairs)  7.54 us
    ppermute x2, starting transfers between devices, per_device(): far = lax.ppermute(onward, 'col', ring)  5.86 us
    ppermute x4, starting transfers between devices, along(): lax.ppermute(array, 'row', [(row_at(y, zl), row_at(y + dy, zl)) for y in...  5.49 us
  transfers between devices with their start and end apart: 37, of which 4 were waited for; matrix products, arithmetic and copies ran while one was open for 7% of the time, Pallas kernels for 10%

profile of v2, /device:TPU:1, one launch (start us, length us, event | category | flops | bytes accessed | tf_op | source)
XLA Modules:
  0.0 166.9 jit_solution(12214594460777668749)
XLA Ops:
  0.0 4.7 %local_part.1 = (bf16[208,1920]{1,0:T(8,128)(2,1)}, bf16[208,1664]{1,0:T(8,128)(2,1)}) custom-call(s32[1]{0:T(128)} %bitcast.6.lane_ref, f32[208,1664]{1,0:T(8,128)} %factor_ref.1), custom_call_target="tpu_custom_call" | custom-call | tf_op jit(solution)/shard_map/local_part/pallas_call | solution.py:90
  7.6 1.6 collective-permute-start.4
  9.1 1.6 collective-permute-start.5
  10.7 1.6 collective-permute-start.6
  14.1 15.8 %prune.1 = (bf16[128,1664]{1,0:T(8,128)(2,1)}, bf16[128,1664]{1,0:T(8,128)(2,1)}, bf16[128,1664]{1,0:T(8,128)(2,1)}, bf16[128,1664]{1,0:T(8,128)(2,1)}, bf16[128...) custom-call(s32[8,13]{1,0:T(8,128)} %keep_ref.1, ...), custom_call_target="tpu_custom_call" | custom-call | tf_op jit(solution)/shard_map/prune/pallas_call | solution.py:172
  32.2 2.5 %collective-permute-start.30 = (bf16[208,1664]{1,0:T(8,128)(2,1)}, bf16[208,1664]{1,0:T(8,128)(2,1)S(1)}, u32[]{:S(2)}, u32[]{:S(2)}) collective-permute-start(bf16[208,1664]{1,0:T(8,128)(2,1)} %get-tuple-element.27), channel_id=1, source_target_pairs={{0,1},{1,0},{2,3},{3,2},{4,5},{5,4},{6,7},{7,6},{8,9},{9,8},{10,11... | collective-permute-start | bytes 2076680 | tf_op jit(solution)/shard_map/ppermute | solution.py:292
  36.8 1.1 add_select_fusion
  41.8 9.1 %collective-permute-done.30 = bf16[208,1664]{1,0:T(8,128)(2,1)S(1)} collective-permute-done((bf16[208,1664]{1,0:T(8,128)(2,1)}, bf16[208,1664]{1,0:T(8,128)(2,1)S(1)}, u32[]{:S(2)}, u32[]{:S(2)}) %collective-permute-start.30) | collective-permute-done | bytes 692256 | tf_op jit(solution)/shard_map/ppermute | solution.py:292
  52.7 2.7 %collective-permute-start.32 = (bf16[416,1664]{1,0:T(8,128)(2,1)S(1)}, bf16[416,1664]{1,0:T(8,128)(2,1)}, u32[]{:S(2)}, u32[]{:S(2)}) collective-permute-start(bf16[416,1664]{1,0:T(8,128)(2,1)S(1)} %pad_maximum_fusion.rest_0_), channel_id=1, source_target_pairs={{0,6},{1,7},{2,0},{3,1},{4,2},{5,3},{6,4},{7,5},{8,14},{9,15},{10,... | collective-permute-start | bytes 4153352 | tf_op jit(solution)/shard_map/ppermute | solution.py:289
  57.0 1.3 collective-permute-start.24
  58.6 1.3 collective-permute-start.14
  59.9 47.5 %collective-permute-done.24 = bf16[128,1664]{1,0:T(8,128)(2,1)S(1)} collective-permute-done((bf16[128,1664]{1,0:T(8,128)(2,1)S(1)}, bf16[128,1664]{1,0:T(8,128)(2,1)S(1)}, u32[]{:S(2)}, u32[]{:S(2)}) %collective-permute-start.24) | collective-permute-done | bytes 426016 | tf_op jit(solution)/shard_map/ppermute | solution.py:324
  107.6 1.4 collective-permute-done.14
  109.8 2.5 %collective-permute-start.15 = (bf16[128,1664]{1,0:T(8,128)(2,1)}, bf16[128,1664]{1,0:T(8,128)(2,1)}, u32[]{:S(2)}, u32[]{:S(2)}) collective-permute-start(bf16[128,1664]{1,0:T(8,128)(2,1)} %broadcast_select_fusion.3.first_ref), channel_id=1, source_target_pairs={{0,64},{16,80},{32,96},{48,112},{64,128},{80,144},{96,160},{112,17... | collective-permute-start | bytes 1277960 | tf_op jit(solution)/shard_map/ppermute | solution.py:326
  114.0 1.3 collective-permute-start.29
  115.3 1.2 slice.33
  116.5 2.8 %collective-permute-start.34 = (bf16[208,1664]{1,0:T(8,128)(2,1)S(1)}, bf16[208,1664]{1,0:T(8,128)(2,1)S(1)}, u32[]{:S(2)}, u32[]{:S(2)}) collective-permute-start(bf16[208,1664]{1,0:T(8,128)(2,1)S(1)} %slice.33), channel_id=1, source_target_pairs={{0,6},{1,7},{2,0},{3,1},{4,2},{5,3},{6,4},{7,5},{8,14},{9,15},{10,... | collective-permute-start | bytes 2076680 | tf_op jit(solution)/shard_map/ppermute | solution.py:289
  119.2 8.8 %collective-permute-start.36 = (bf16[128,1664]{1,0:T(8,128)(2,1)}, bf16[128,1664]{1,0:T(8,128)(2,1)}, u32[]{:S(2)}, u32[]{:S(2)}) collective-permute-start(bf16[128,1664]{1,0:T(8,128)(2,1)} %collective-permute-done.25.rest_1_), channel_id=1, source_target_pairs={{0,8},{8,0},{16,24},{24,16},{32,40},{40,32},{48,56},{56,48},{64,72... | collective-permute-start | bytes 1277960 | tf_op jit(solution)/shard_map/ppermute | solution.py:332
  130.2 5.8 %collective-permute-start.16 = (bf16[64,1664]{1,0:T(8,128)(2,1)S(1)}, bf16[64,1664]{1,0:T(8,128)(2,1)}, u32[]{:S(2)}, u32[]{:S(2)}) collective-permute-start(bf16[64,1664]{1,0:T(8,128)(2,1)S(1)} %constant_dynamic-slice_fusion.1), channel_id=1, source_target_pairs={{0,64},{16,80},{32,96},{48,112},{64,128},{80,144},{96,160},{112,17... | collective-permute-start | bytes 638984 | tf_op jit(solution)/shard_map/ppermute | solution.py:328
  136.0 1.7 %collective-permute-start.28 = (bf16[64,1664]{1,0:T(8,128)(2,1)S(1)}, bf16[64,1664]{1,0:T(8,128)(2,1)}, u32[]{:S(2)}, u32[]{:S(2)}) collective-permute-start(bf16[64,1664]{1,0:T(8,128)(2,1)S(1)} %collective-permute-done.26.rest_1_), channel_id=1, source_target_pairs={{0,8},{8,0},{16,24},{24,16},{32,40},{40,32},{48,56},{56,48},{64,72... | collective-permute-start | bytes 638984 | tf_op jit(solution)/shard_map/ppermute | solution.py:333
  138.7 2.6 %collective-permute-start.27 = (bf16[64,1664]{1,0:T(8,128)(2,1)}, bf16[64,1664]{1,0:T(8,128)(2,1)}, u32[]{:S(2)}, u32[]{:S(2)}) collective-permute-start(bf16[64,1664]{1,0:T(8,128)(2,1)} %collective-permute-done.16.rest_0_), channel_id=1, source_target_pairs={{0,8},{8,0},{16,24},{24,16},{32,40},{40,32},{48,56},{56,48},{64,72... | collective-permute-start | bytes 638984 | tf_op jit(solution)/shard_map/ppermute | solution.py:333
  144.0 7.1 %shard_map.37 = (bf16[1024,1664]{1,0:T(8,128)(2,1)}, bf16[1664,1664]{1,0:T(8,128)(2,1)}) custom-call(s32[7]{0:T(128)} %stack.106.at_ref, bf16[128,1664]{1,0:T(8,128)(2,1)} %broadcast_select_fusion.3.first_ref, bf16[128,1664]{1,0:T(8,128)(2,1)} %copy-done.2, bf16[16,128]{1,0:T(8,128)(2,1)} %copy-done.10, ...), custom_call_target="tpu_custom_call", output_to_operand_aliasing={{0}: (10, {})} | custom-call | tf_op jit(solution)/shard_map/pallas_call | solution.py:229
  151.1 8.9 %shard_map.38.rest_6_ = bf16[1024,1664]{1,0:T(8,128)(2,1)} custom-call(s32[3]{0:T(128)} %pad_add_fusion.at_ref, bf16[128,1664]{1,0:T(8,128)(2,1)} %collective-permute-done.15.rest_0_, bf16[128,1664]{1,0:T(8,128)(2,1)} %collective-permute-done.25.rest_1_, bf16[128,1664]{1,0:T(8,128)(2,1)} %collective-permute-done.35.rest_2_, ...), custom_call_target="tpu_custom_call", output_to_operand_aliasing={{}: (7, {})} | custom-call | tf_op jit(solution)/shard_map/pallas_call | solution.py:229
  160.1 6.8 %shard_map.39 = bf16[1024,1664]{1,0:T(8,128)(2,1)} custom-call(s32[6]{0:T(128)} %stack.90.at_ref, bf16[64,1664]{1,0:T(8,128)(2,1)} %collective-permute-done.16.rest_0_, bf16[64,1664]{1,0:T(8,128)(2,1)} %copy-done.9, bf16[64,1664]{1,0:T(8,128)(2,1)} %collective-permute-done.27.rest_2_, ...), custom_call_target="tpu_custom_call", output_to_operand_aliasing={{}: (7, {})} | custom-call | tf_op jit(solution)/shard_map/pallas_call | solution.py:229
  (98 shorter events, 24.8 us)
Async XLA Ops:
  6.1 6.8 %collective-permute-start.2 = (bf16[208,1920]{1,0:T(8,128)(2,1)}, bf16[208,1920]{1,0:T(8,128)(2,1)S(1)}, u32[]{:S(2)}, u32[]{:S(2)}) collective-permute-start(bf16[208,1920]{1,0:T(8,128)(2,1)} %get-tuple-element.18.rest_0_), channel_id=1, source_target_pairs={{0,3},{1,2},{2,5},{3,4},{4,7},{5,6},{6,1},{7,0}} | collective-permute-start | bytes 2396168 | tf_op jit(solution)/shard_map/ppermute | solution.py:265
  6.9 6.1 %collective-permute-start.3 = (bf16[208,1920]{1,0:T(8,128)(2,1)}, bf16[208,1920]{1,0:T(8,128)(2,1)S(1)}, u32[]{:S(2)}, u32[]{:S(2)}) collective-permute-start(bf16[208,1920]{1,0:T(8,128)(2,1)} %get-tuple-element.18.rest_0_), channel_id=1, source_target_pairs={{0,6},{1,7},{2,0},{3,1},{4,2},{5,3},{6,4},{7,5}} | collective-permute-start | bytes 2396168 | tf_op jit(solution)/shard_map/ppermute | solution.py:265
  7.6 5.4 %collective-permute-start.4 = (bf16[208,1920]{1,0:T(8,128)(2,1)}, bf16[208,1920]{1,0:T(8,128)(2,1)}, u32[]{:S(2)}, u32[]{:S(2)}) collective-permute-start(bf16[208,1920]{1,0:T(8,128)(2,1)} %get-tuple-element.18.rest_0_), channel_id=1, source_target_pairs={{0,1},{1,0},{2,3},{3,2},{4,5},{5,4},{6,7},{7,6}} | collective-permute-start | bytes 2396168 | tf_op jit(solution)/shard_map/ppermute | solution.py:265
  29.9 5.4 %collective-permute-start.17 = (bf16[128,1664]{1,0:T(8,128)(2,1)}, bf16[128,1664]{1,0:T(8,128)(2,1)S(1)}, u32[]{:S(2)}, u32[]{:S(2)}) collective-permute-start(bf16[128,1664]{1,0:T(8,128)(2,1)} %get-tuple-element.24), channel_id=1, source_target_pairs={{0,128},{1,129},{2,130},{3,131},{4,132},{5,133},{6,134},{7,135}} | collective-permute-start | bytes 1277960 | tf_op jit(solution)/shard_map/ppermute | solution.py:315
  32.2 18.8 %collective-permute-start.30 = (bf16[208,1664]{1,0:T(8,128)(2,1)}, bf16[208,1664]{1,0:T(8,128)(2,1)S(1)}, u32[]{:S(2)}, u32[]{:S(2)}) collective-permute-start(bf16[208,1664]{1,0:T(8,128)(2,1)} %get-tuple-element.27), channel_id=1, source_target_pairs={{0,1},{1,0},{2,3},{3,2},{4,5},{5,4},{6,7},{7,6},{8,9},{9,8},{10,11... | collective-permute-start | bytes 2076680 | tf_op jit(solution)/shard_map/ppermute | solution.py:292
  37.9 13.1 %collective-permute-start.20 = (bf16[128,1664]{1,0:T(8,128)(2,1)S(1)}, bf16[128,1664]{1,0:T(8,128)(2,1)S(1)}, u32[]{:S(2)}, u32[]{:S(2)}) collective-permute-start(bf16[128,1664]{1,0:T(8,128)(2,1)S(1)} %add_select_fusion), channel_id=1, source_target_pairs={{0,16},{64,80},{128,144},{192,208},{1,17},{65,81},{129,145},{193,2... | collective-permute-start | bytes 1277960 | tf_op jit(solution)/shard_map/ppermute | solution.py:318
  38.6 13.2 %collective-permute-start.21 = (bf16[128,1664]{1,0:T(8,128)(2,1)S(1)}, bf16[128,1664]{1,0:T(8,128)(2,1)S(1)}, u32[]{:S(2)}, u32[]{:S(2)}) collective-permute-start(bf16[128,1664]{1,0:T(8,128)(2,1)S(1)} %add_select_fusion), channel_id=1, source_target_pairs={{0,48},{64,112},{128,176},{192,240},{1,49},{65,113},{129,177},{193... | collective-permute-start | bytes 1277960 | tf_op jit(solution)/shard_map/ppermute | solution.py:319
  40.5 12.3 %collective-permute-start.10 = (bf16[128,1664]{1,0:T(8,128)(2,1)S(1)}, bf16[128,1664]{1,0:T(8,128)(2,1)S(1)}, u32[]{:S(2)}, u32[]{:S(2)}) collective-permute-start(bf16[128,1664]{1,0:T(8,128)(2,1)S(1)} %add_select_fusion.1), channel_id=1, source_target_pairs={{0,16},{64,80},{128,144},{192,208},{1,17},{65,81},{129,145},{193,2... | collective-permute-start | bytes 1277960 | tf_op jit(solution)/shard_map/ppermute | solution.py:318
  41.1 14.3 %collective-permute-start.11 = (bf16[128,1664]{1,0:T(8,128)(2,1)S(1)}, bf16[128,1664]{1,0:T(8,128)(2,1)S(1)}, u32[]{:S(2)}, u32[]{:S(2)}) collective-permute-start(bf16[128,1664]{1,0:T(8,128)(2,1)S(1)} %add_select_fusion.1), channel_id=1, source_target_pairs={{0,48},{64,112},{128,176},{192,240},{1,49},{65,113},{129,177},{193... | collective-permute-start | bytes 1277960 | tf_op jit(solution)/shard_map/ppermute | solution.py:319
  52.6 59.7 %collective-permute-start.31 = (bf16[416,1664]{1,0:T(8,128)(2,1)S(1)}, bf16[416,1664]{1,0:T(8,128)(2,1)S(1)}, u32[]{:S(2)}, u32[]{:S(2)}) collective-permute-start(bf16[416,1664]{1,0:T(8,128)(2,1)S(1)} %pad_maximum_fusion.rest_0_), channel_id=1, source_target_pairs={{0,2},{1,3},{2,4},{3,5},{4,6},{5,7},{6,0},{7,1},{8,10},{9,11},{10,... | collective-permute-start | bytes 4153352 | tf_op jit(solution)/shard_map/ppermute | solution.py:289
  52.7 62.6 %collective-permute-start.32 = (bf16[416,1664]{1,0:T(8,128)(2,1)S(1)}, bf16[416,1664]{1,0:T(8,128)(2,1)}, u32[]{:S(2)}, u32[]{:S(2)}) collective-permute-start(bf16[416,1664]{1,0:T(8,128)(2,1)S(1)} %pad_maximum_fusion.rest_0_), channel_id=1, source_target_pairs={{0,6},{1,7},{2,0},{3,1},{4,2},{5,3},{6,4},{7,5},{8,14},{9,15},{10,... | collective-permute-start | bytes 4153352 | tf_op jit(solution)/shard_map/ppermute | solution.py:289
  57.0 50.4 %collective-permute-start.24 = (bf16[128,1664]{1,0:T(8,128)(2,1)S(1)}, bf16[128,1664]{1,0:T(8,128)(2,1)S(1)}, u32[]{:S(2)}, u32[]{:S(2)}) collective-permute-start(bf16[128,1664]{1,0:T(8,128)(2,1)S(1)} %fusion.1), channel_id=1, source_target_pairs={{0,8},{16,24},{32,40},{48,56},{64,72},{80,88},{96,104},{112,120},{... | collective-permute-start | bytes 1277960 | tf_op jit(solution)/shard_map/ppermute | solution.py:324
  58.6 50.4 %collective-permute-start.14 = (bf16[128,1664]{1,0:T(8,128)(2,1)S(1)}, bf16[128,1664]{1,0:T(8,128)(2,1)S(1)}, u32[]{:S(2)}, u32[]{:S(2)}) collective-permute-start(bf16[128,1664]{1,0:T(8,128)(2,1)S(1)} %fusion), channel_id=1, source_target_pairs={{0,8},{16,24},{32,40},{48,56},{64,72},{80,88},{96,104},{112,120},{... | collective-permute-start | bytes 1277960 | tf_op jit(solution)/shard_map/ppermute | solution.py:324
  107.5 11.7 %collective-permute-start.25 = (bf16[128,1664]{1,0:T(8,128)(2,1)S(1)}, bf16[128,1664]{1,0:T(8,128)(2,1)}, u32[]{:S(2)}, u32[]{:S(2)}) collective-permute-start(bf16[128,1664]{1,0:T(8,128)(2,1)S(1)} %broadcast_select_fusion.2.second_ref), channel_id=1, source_target_pairs={{0,64},{16,80},{32,96},{48,112},{64,128},{80,144},{96,160},{112,17... | collective-permute-start | bytes 1277960 | tf_op jit(solution)/shard_map/ppermute | solution.py:326
  109.8 18.2 %collective-permute-start.15 = (bf16[128,1664]{1,0:T(8,128)(2,1)}, bf16[128,1664]{1,0:T(8,128)(2,1)}, u32[]{:S(2)}, u32[]{:S(2)}) collective-permute-start(bf16[128,1664]{1,0:T(8,128)(2,1)} %broadcast_select_fusion.3.first_ref), channel_id=1, source_target_pairs={{0,64},{16,80},{32,96},{48,112},{64,128},{80,144},{96,160},{112,17... | collective-permute-start | bytes 1277960 | tf_op jit(solution)/shard_map/ppermute | solution.py:326
  113.3 16.9 %collective-permute-start.33 = (bf16[208,1664]{1,0:T(8,128)(2,1)}, bf16[208,1664]{1,0:T(8,128)(2,1)}, u32[]{:S(2)}, u32[]{:S(2)}) collective-permute-start(bf16[208,1664]{1,0:T(8,128)(2,1)} %slice.32), channel_id=1, source_target_pairs={{0,2},{1,3},{2,4},{3,5},{4,6},{5,7},{6,0},{7,1},{8,10},{9,11},{10,... | collective-permute-start | bytes 2076680 | tf_op jit(solution)/shard_map/ppermute | solution.py:289
  114.0 16.1 %collective-permute-start.29 = (bf16[16,128]{1,0:T(8,128)(2,1)S(1)}, bf16[16,128]{1,0:T(8,128)(2,1)S(1)}, u32[]{:S(2)}, u32[]{:S(2)}) collective-permute-start(bf16[16,128]{1,0:T(8,128)(2,1)S(1)} %slice.25), channel_id=1, source_target_pairs={{0,8},{1,9},{2,10},{3,11},{4,12},{5,13},{6,14},{7,15}} | collective-permute-start | bytes 12296 | tf_op jit(solution)/shard_map/ppermute | solution.py:291
  116.5 26.7 %collective-permute-start.34 = (bf16[208,1664]{1,0:T(8,128)(2,1)S(1)}, bf16[208,1664]{1,0:T(8,128)(2,1)S(1)}, u32[]{:S(2)}, u32[]{:S(2)}) collective-permute-start(bf16[208,1664]{1,0:T(8,128)(2,1)S(1)} %slice.33), channel_id=1, source_target_pairs={{0,6},{1,7},{2,0},{3,1},{4,2},{5,3},{6,4},{7,5},{8,14},{9,15},{10,... | collective-permute-start | bytes 2076680 | tf_op jit(solution)/shard_map/ppermute | solution.py:289
  119.2 31.9 %collective-permute-start.36 = (bf16[128,1664]{1,0:T(8,128)(2,1)}, bf16[128,1664]{1,0:T(8,128)(2,1)}, u32[]{:S(2)}, u32[]{:S(2)}) collective-permute-start(bf16[128,1664]{1,0:T(8,128)(2,1)} %collective-permute-done.25.rest_1_), channel_id=1, source_target_pairs={{0,8},{8,0},{16,24},{24,16},{32,40},{40,32},{48,56},{56,48},{64,72... | collective-permute-start | bytes 1277960 | tf_op jit(solution)/shard_map/ppermute | solution.py:332
  128.0 23.1 %collective-permute-start.35 = (bf16[128,1664]{1,0:T(8,128)(2,1)}, bf16[128,1664]{1,0:T(8,128)(2,1)}, u32[]{:S(2)}, u32[]{:S(2)}) collective-permute-start(bf16[128,1664]{1,0:T(8,128)(2,1)} %collective-permute-done.15.rest_0_), channel_id=1, source_target_pairs={{0,8},{8,0},{16,24},{24,16},{32,40},{40,32},{48,56},{56,48},{64,72... | collective-permute-start | bytes 1277960 | tf_op jit(solution)/shard_map/ppermute | solution.py:332
  130.1 5.9 %collective-permute-start.26 = (bf16[64,1664]{1,0:T(8,128)(2,1)S(1)}, bf16[64,1664]{1,0:T(8,128)(2,1)S(1)}, u32[]{:S(2)}, u32[]{:S(2)}) collective-permute-start(bf16[64,1664]{1,0:T(8,128)(2,1)S(1)} %constant_dynamic-slice_fusion), channel_id=1, source_target_pairs={{0,64},{16,80},{32,96},{48,112},{64,128},{80,144},{96,160},{112,17... | collective-permute-start | bytes 638984 | tf_op jit(solution)/shard_map/ppermute | solution.py:328
  130.2 8.6 %collective-permute-start.16 = (bf16[64,1664]{1,0:T(8,128)(2,1)S(1)}, bf16[64,1664]{1,0:T(8,128)(2,1)}, u32[]{:S(2)}, u32[]{:S(2)}) collective-permute-start(bf16[64,1664]{1,0:T(8,128)(2,1)S(1)} %constant_dynamic-slice_fusion.1), channel_id=1, source_target_pairs={{0,64},{16,80},{32,96},{48,112},{64,128},{80,144},{96,160},{112,17... | collective-permute-start | bytes 638984 | tf_op jit(solution)/shard_map/ppermute | solution.py:328
  136.0 24.1 %collective-permute-start.28 = (bf16[64,1664]{1,0:T(8,128)(2,1)S(1)}, bf16[64,1664]{1,0:T(8,128)(2,1)}, u32[]{:S(2)}, u32[]{:S(2)}) collective-permute-start(bf16[64,1664]{1,0:T(8,128)(2,1)S(1)} %collective-permute-done.26.rest_1_), channel_id=1, source_target_pairs={{0,8},{8,0},{16,24},{24,16},{32,40},{40,32},{48,56},{56,48},{64,72... | collective-permute-start | bytes 638984 | tf_op jit(solution)/shard_map/ppermute | solution.py:333
  138.7 21.3 %collective-permute-start.27 = (bf16[64,1664]{1,0:T(8,128)(2,1)}, bf16[64,1664]{1,0:T(8,128)(2,1)}, u32[]{:S(2)}, u32[]{:S(2)}) collective-permute-start(bf16[64,1664]{1,0:T(8,128)(2,1)} %collective-permute-done.16.rest_0_), channel_id=1, source_target_pairs={{0,8},{8,0},{16,24},{24,16},{32,40},{40,32},{48,56},{56,48},{64,72... | collective-permute-start | bytes 638984 | tf_op jit(solution)/shard_map/ppermute | solution.py:333
  (24 other events, 241.4 us)

commit v3 on v2

--- a/solution.py
+++ b/solution.py
@@ -191,8 +191,8 @@
 
 
 def own_kernel(at_ref, first_ref, second_ref, token_ref, *rest):
-    parts = rest[:5]
-    weight_ref, kept_ref, out_ref, factor_ref = rest[5:]
+    parts = rest[:LANES]
+    weight_ref, kept_ref, out_ref, factor_ref = rest[LANES:]
     for place, part in enumerate(parts):
         start = pl.multiple_of(at_ref[2 + place] * LANE_ROWS, 16)
         factor_ref[pl.ds(start, part.shape[0]), :] = part[...]
@@ -285,23 +285,27 @@
     ]
     *parts_out, kept = prune(keep_mask, jnp.stack(order).astype(jnp.int32), weight, pieces)
 
-    def along(array, dy):
-        return lax.ppermute(array, "row", [(row_at(y, zl), row_at(y + dy, zl)) for y in range(4) for zl in (0, 1)])
+    def along(array, dy, flip=0):
+        pairs = [
+            (c * LANES + row_at(y, zl), c * LANES + row_at(y + dy, zl ^ flip))
+            for c in range(1, 32)
+            for y in range(4)
+            for zl in (0, 1)
+        ]
+        return lax.ppermute(array, ("col", "row"), pairs)
 
     token = lax.ppermute(factor_low[:16, :BLK], "col", [(0, 1)])
-    partner = lax.ppermute(factor_low, "row", [(k, k ^ 1) for k in range(LANES)])
-    even = zl_at == 0
-    pair = jnp.concatenate(
-        [jnp.where(even, factor_low, partner), jnp.where(even, partner, factor_low)], axis=0
-    )
-    pair_up = along(pair, 1)
-    pair_down = along(pair, 3)
-    far_even = along(pair_up[:LANE_ROWS], 1)
-    far_odd = along(pair_down[LANE_ROWS:], 3)
-    parts = (pair, pair_up, pair_down, far_even, far_odd)
-    part_rows = [
-        row_at(y_at, 0), row_at(y_at + 3, 0), row_at(y_at + 1, 0), row_at(y_at + 2, 0), row_at(y_at + 2, 1)
-    ]
+    partner = along(factor_low, 0, 1)
+    even = jnp.where(zl_at == 0, factor_low, partner)
+    odd = jnp.where(zl_at == 0, partner, factor_low)
+    even_up = along(even, 1)
+    odd_down = along(odd, 3)
+    odd_up = along(odd, 1)
+    even_down = along(even, 3)
+    even_far = along(even_up, 1)
+    odd_far = along(odd_down, 3)
+    parts = (even, odd, even_up, odd_up, even_down, odd_down, even_far, odd_far)
+    part_rows = [row_at(y_at + dy, zl) for dy in (0, 3, 1, 2) for zl in (0, 1)]
 
     places = [(x, z) for x in range(4) for z in range(4)]
     share = [(col_at(x, z, 0), col_at(x, z, 1)) for x, z in places]
@@ -317,9 +321,9 @@
         own = jnp.where(x_at == 0, parts_out[chunk], got)
         up = lax.ppermute(own, "col", [(col_at(x, 0, 0), col_at(x, 1, 0)) for x in range(4)])
         down = lax.ppermute(own, "col", [(col_at(x, 0, 0), col_at(x, 3, 0)) for x in range(4)])
-        far_a = lax.ppermute(up[:FORWARD], "col", [(col_at(x, 1, 0), col_at(x, 2, 0)) for x in range(4)])
-        far_b = lax.ppermute(down[FORWARD:], "col", [(col_at(x, 3, 0), col_at(x, 2, 0)) for x in range(4)])
-        own = jnp.where(zh_at == 0, own, up + down + jnp.concatenate([far_a, far_b], axis=0))
+        side, array = ((1, up), (3, down))[chunk]
+        far_z = lax.ppermute(array, "col", [(col_at(x, side, 0), col_at(x, 2, 0)) for x in range(4)])
+        own = jnp.where(zh_at == 0, own, up + down + far_z)
 
         shared = lax.ppermute(own, "col", share)
         own = jnp.where(core_at == 0, own, shared)
@@ -357,4 +361,6 @@
 def solution(mesh):
     in_specs = (P("row", "col"), P("row", "col"), P("row", None))
     out_specs = P("row", "col")
-    return jax.shard_map(per_device, mesh=mesh, in_specs=in_specs, out_specs=out_specs, check_vma=False)
+    return jax.shard_map(
+        per_device, mesh=mesh, in_specs=in_specs, out_specs=out_specs, check_vma=False
+    )

time: 169 us -> 177 us (1.047)
  waiting for transfers between devices: 59.2 us -> 65.7 us
  other arithmetic: 4.42 us -> 6.53 us
  starting transfers between devices: 50.7 us -> 52.7 us
    ppermute x9, starting transfers between devices: 10.7 us -> 25 us  [the longest x7 22.9 us: along(): return lax.ppermute(array, ('col', 'row'), pairs)]
    ppermute x2, starting transfers between devices: 8.92 us -> 0.51 us  [per_device(): near_others.append(lax.ppermute(near, 'col', swap))]
    ppermute x2, starting transfers between devices: 5.86 us -> 0.4 us  [per_device(): far = lax.ppermute(onward, 'col', ring)]
    ppermute x2, waiting for transfers between devices: 0.01 us -> 4.09 us  [per_device(): near = lax.ppermute(own, 'col', ring)]
    ppermute x2, waiting for transfers between devices: 1.12 us -> 4.63 us  [per_device(): far = lax.ppermute(onward, 'col', ring)]
    select_n x3, other arithmetic: 0.6 us -> 3.62 us  [the longest x2 2.39 us: per_device(): own = jnp.where(zh_at == 0, own, up + down + far_z)]
    unnamed x22 -> x38, local copies, waits for them, and re-layouts: 1.99 us -> 4.34 us
    ppermute x9, waiting for transfers between devices: 9.09 us -> 6.78 us  [the longest x7 6.77 us: along(): return lax.ppermute(array, ('col', 'row'), pairs)]
  transfers between devices with their start and end apart: 37 -> 37, of which waited for: 4 -> 7; matrix products, arithmetic and copies ran while one was open for 7% -> 5% of each run, Pallas kernels for 10% -> 9%
where the time goes in v3:
time: 177 us; the launch traced here: 176 us
  waiting for transfers between devices  65.7 us (37%)
  starting transfers between devices  52.7 us (30%)
  Pallas kernels  43.4 us (25%)
  local copies, waits for them, and re-layouts  6.98 us (4%)
  other arithmetic  6.53 us (4%)
    ppermute x2, waiting for transfers between devices, per_device(): shared = lax.ppermute(own, 'col', share)  48.4 us
    ppermute x7, starting transfers between devices, along(): return lax.ppermute(array, ('col', 'row'), pairs)  22.9 us
    pallas_call x3, Pallas kernels, finish(): pl.pallas_call(kernel, grid_spec=pltpu.PrefetchScalarGridSpec(num_scalar_...  22.8 us
    pallas_call x1, Pallas kernels, prune(): pl.pallas_call(prune_kernel, in_specs=[smem, smem, hbm] + [hbm] * LANES,...  15.8 us
    ppermute x7, starting transfers between devices, hop(): return lax.ppermute(array, ('col', 'row'), pairs)  7.53 us
    ppermute x7, waiting for transfers between devices, along(): return lax.ppermute(array, ('col', 'row'), pairs)  6.77 us
    pallas_call x1, Pallas kernels, local_part(): pl.pallas_call(local_kernel, in_specs=[smem, vmem], out_specs=(vmem, vmem...  4.74 us
    ppermute x2, waiting for transfers between devices, per_device(): far = lax.ppermute(onward, 'col', ring)  4.63 us
  transfers between devices with their start and end apart: 37, of which 7 were waited for; matrix products, arithmetic and copies ran while one was open for 5% of the time, Pallas kernels for 9%

profile of v3, /device:TPU:1, one launch (start us, length us, event | category | flops | bytes accessed | tf_op | source)
XLA Modules:
  0.0 175.9 jit_solution(12899684711653958717)
XLA Ops:
  0.0 4.7 %local_part.1 = (bf16[208,1920]{1,0:T(8,128)(2,1)}, bf16[208,1664]{1,0:T(8,128)(2,1)}) custom-call(s32[1]{0:T(128)} %bitcast.6.lane_ref, f32[208,1664]{1,0:T(8,128)} %factor_ref.1), custom_call_target="tpu_custom_call" | custom-call | tf_op jit(solution)/shard_map/local_part/pallas_call | solution.py:90
  7.6 1.6 collective-permute-start.4
  9.2 1.6 collective-permute-start.5
  10.8 1.6 collective-permute-start.6
  14.1 15.8 %prune.1 = (bf16[128,1664]{1,0:T(8,128)(2,1)}, bf16[128,1664]{1,0:T(8,128)(2,1)}, bf16[128,1664]{1,0:T(8,128)(2,1)}, bf16[128,1664]{1,0:T(8,128)(2,1)}, bf16[128...) custom-call(s32[8,13]{1,0:T(8,128)} %keep_ref.1, ...), custom_call_target="tpu_custom_call" | custom-call | tf_op jit(solution)/shard_map/prune/pallas_call | solution.py:172
  32.2 4.4 %collective-permute-start.28 = (bf16[208,1664]{1,0:T(8,128)(2,1)}, bf16[208,1664]{1,0:T(8,128)(2,1)}, u32[]{:S(2)}, u32[]{:S(2)}) collective-permute-start(bf16[208,1664]{1,0:T(8,128)(2,1)} %get-tuple-element.27), channel_id=1, source_target_pairs={{8,9},{9,8},{10,11},{11,10},{12,13},{13,12},{14,15},{15,14},{16,17... | collective-permute-start | bytes 2076680 | tf_op jit(solution)/shard_map/ppermute | solution.py:295
  45.9 4.9 %collective-permute-done.28 = bf16[208,1664]{1,0:T(8,128)(2,1)} collective-permute-done((bf16[208,1664]{1,0:T(8,128)(2,1)}, bf16[208,1664]{1,0:T(8,128)(2,1)}, u32[]{:S(2)}, u32[]{:S(2)}) %collective-permute-start.28) | collective-permute-done | bytes 692256 | tf_op jit(solution)/shard_map/ppermute | solution.py:295
  52.0 1.9 %collective-permute-start.29 = (bf16[208,1664]{1,0:T(8,128)(2,1)S(1)}, bf16[208,1664]{1,0:T(8,128)(2,1)}, u32[]{:S(2)}, u32[]{:S(2)}) collective-permute-start(bf16[208,1664]{1,0:T(8,128)(2,1)S(1)} %get-tuple-element.32.rest_0_), channel_id=1, source_target_pairs={{8,10},{9,11},{10,12},{11,13},{12,14},{13,15},{14,8},{15,9},{16,18... | collective-permute-start | bytes 2076680 | tf_op jit(solution)/shard_map/ppermute | solution.py:295
  54.0 4.6 %collective-permute-start.32 = (bf16[208,1664]{1,0:T(8,128)(2,1)S(1)}, bf16[208,1664]{1,0:T(8,128)(2,1)S(1)}, u32[]{:S(2)}, u32[]{:S(2)}) collective-permute-start(bf16[208,1664]{1,0:T(8,128)(2,1)S(1)} %get-tuple-element.31.rest_1_), channel_id=1, source_target_pairs={{8,14},{9,15},{10,8},{11,9},{12,10},{13,11},{14,12},{15,13},{16,22... | collective-permute-start | bytes 2076680 | tf_op jit(solution)/shard_map/ppermute | solution.py:295
  58.5 1.9 %collective-permute-start.30 = (bf16[208,1664]{1,0:T(8,128)(2,1)S(1)}, bf16[208,1664]{1,0:T(8,128)(2,1)}, u32[]{:S(2)}, u32[]{:S(2)}) collective-permute-start(bf16[208,1664]{1,0:T(8,128)(2,1)S(1)} %get-tuple-element.31.rest_1_), channel_id=1, source_target_pairs={{8,10},{9,11},{10,12},{11,13},{12,14},{13,15},{14,8},{15,9},{16,18... | collective-permute-start | bytes 2076680 | tf_op jit(solution)/shard_map/ppermute | solution.py:295
  63.2 1.9 %collective-permute-done.29.rest_2_ = bf16[208,1664]{1,0:T(8,128)(2,1)} collective-permute-done((bf16[208,1664]{1,0:T(8,128)(2,1)S(1)}, bf16[208,1664]{1,0:T(8,128)(2,1)}, u32[]{:S(2)}, u32[]{:S(2)}) %collective-permute-start.29) | collective-permute-done | bytes 692256 | tf_op jit(solution)/shard_map/ppermute | solution.py:295
  65.0 2.7 %collective-permute-start.31 = (bf16[208,1664]{1,0:T(8,128)(2,1)S(1)}, bf16[208,1664]{1,0:T(8,128)(2,1)}, u32[]{:S(2)}, u32[]{:S(2)}) collective-permute-start(bf16[208,1664]{1,0:T(8,128)(2,1)S(1)} %get-tuple-element.32.rest_0_), channel_id=1, source_target_pairs={{8,14},{9,15},{10,8},{11,9},{12,10},{13,11},{14,12},{15,13},{16,22... | collective-permute-start | bytes 2076680 | tf_op jit(solution)/shard_map/ppermute | solution.py:295
  67.8 2.6 %collective-permute-start.33 = (bf16[208,1664]{1,0:T(8,128)(2,1)}, bf16[208,1664]{1,0:T(8,128)(2,1)}, u32[]{:S(2)}, u32[]{:S(2)}) collective-permute-start(bf16[208,1664]{1,0:T(8,128)(2,1)} %collective-permute-done.29.rest_2_), channel_id=1, source_target_pairs={{8,10},{9,11},{10,12},{11,13},{12,14},{13,15},{14,8},{15,9},{16,18... | collective-permute-start | bytes 2076680 | tf_op jit(solution)/shard_map/ppermute | solution.py:295
  72.8 46.2 %collective-permute-done.22 = bf16[128,1664]{1,0:T(8,128)(2,1)S(1)} collective-permute-done((bf16[128,1664]{1,0:T(8,128)(2,1)S(1)}, bf16[128,1664]{1,0:T(8,128)(2,1)S(1)}, u32[]{:S(2)}, u32[]{:S(2)}) %collective-permute-start.22) | collective-permute-done | bytes 426016 | tf_op jit(solution)/shard_map/ppermute | solution.py:328
  120.3 2.3 %collective-permute-done.13 = bf16[128,1664]{1,0:T(8,128)(2,1)S(1)} collective-permute-done((bf16[128,1664]{1,0:T(8,128)(2,1)S(1)}, bf16[128,1664]{1,0:T(8,128)(2,1)S(1)}, u32[]{:S(2)}, u32[]{:S(2)}) %collective-permute-start.13) | collective-permute-done | bytes 426016 | tf_op jit(solution)/shard_map/ppermute | solution.py:328
  126.7 4.1 %collective-permute-done.23.rest_1_ = bf16[128,1664]{1,0:T(8,128)(2,1)S(1)} collective-permute-done((bf16[128,1664]{1,0:T(8,128)(2,1)S(1)}, bf16[128,1664]{1,0:T(8,128)(2,1)S(1)}, u32[]{:S(2)}, u32[]{:S(2)}) %collective-permute-start.23) | collective-permute-done | bytes 426016 | tf_op jit(solution)/shard_map/ppermute | solution.py:330
  130.8 4.8 %collective-permute-start.34 = (bf16[208,1664]{1,0:T(8,128)(2,1)}, bf16[208,1664]{1,0:T(8,128)(2,1)}, u32[]{:S(2)}, u32[]{:S(2)}) collective-permute-start(bf16[208,1664]{1,0:T(8,128)(2,1)} %copy-done.11), channel_id=1, source_target_pairs={{8,14},{9,15},{10,8},{11,9},{12,10},{13,11},{14,12},{15,13},{16,22... | collective-permute-start | bytes 2076680 | tf_op jit(solution)/shard_map/ppermute | solution.py:295
  137.1 1.7 collective-permute-done.27.token_ref
  139.7 4.6 %collective-permute-done.24.rest_1_ = bf16[64,1664]{1,0:T(8,128)(2,1)S(1)} collective-permute-done((bf16[64,1664]{1,0:T(8,128)(2,1)S(1)}, bf16[64,1664]{1,0:T(8,128)(2,1)S(1)}, u32[]{:S(2)}, u32[]{:S(2)}) %collective-permute-start.24) | collective-permute-done | bytes 213024 | tf_op jit(solution)/shard_map/ppermute | solution.py:332
  144.3 2.2 %collective-permute-start.26 = (bf16[64,1664]{1,0:T(8,128)(2,1)S(1)}, bf16[64,1664]{1,0:T(8,128)(2,1)S(1)}, u32[]{:S(2)}, u32[]{:S(2)}) collective-permute-start(bf16[64,1664]{1,0:T(8,128)(2,1)S(1)} %collective-permute-done.24.rest_1_), channel_id=1, source_target_pairs={{0,8},{8,0},{16,24},{24,16},{32,40},{40,32},{48,56},{56,48},{64,72... | collective-permute-start | bytes 638984 | tf_op jit(solution)/shard_map/ppermute | solution.py:337
  146.6 2.2 %collective-permute-start.25 = (bf16[64,1664]{1,0:T(8,128)(2,1)S(1)}, bf16[64,1664]{1,0:T(8,128)(2,1)S(1)}, u32[]{:S(2)}, u32[]{:S(2)}) collective-permute-start(bf16[64,1664]{1,0:T(8,128)(2,1)S(1)} %collective-permute-done.15.rest_0_), channel_id=1, source_target_pairs={{0,8},{8,0},{16,24},{24,16},{32,40},{40,32},{48,56},{56,48},{64,72... | collective-permute-start | bytes 638984 | tf_op jit(solution)/shard_map/ppermute | solution.py:337
  150.7 7.1 %shard_map.37 = (bf16[1024,1664]{1,0:T(8,128)(2,1)}, bf16[1664,1664]{1,0:T(8,128)(2,1)}) custom-call(s32[10]{0:T(128)} %stack.118.at_ref, bf16[128,1664]{1,0:T(8,128)(2,1)} %copy-done.3, bf16[128,1664]{1,0:T(8,128)(2,1)} %copy-done.2, bf16[16,128]{1,0:T(8,128)(2,1)} %copy-done.18, bf16[208,1664]{1,0:T(8,128)(2,1)} %copy-done.1, ...), custom_call_target="tpu_custom_call", output_to_operand_aliasing={{0}: (13, {})} | custom-call | tf_op jit(solution)/shard_map/pallas_call | solution.py:229
  158.8 8.9 %shard_map.38.rest_6_ = bf16[1024,1664]{1,0:T(8,128)(2,1)} custom-call(s32[3]{0:T(128)} %pad_add_fusion.at_ref, bf16[128,1664]{1,0:T(8,128)(2,1)} %copy-done.5, bf16[128,1664]{1,0:T(8,128)(2,1)} %copy-done.4, bf16[128,1664]{1,0:T(8,128)(2,1)} %copy-done.13, bf16[128,1664]{1,0:T(8,128)(2,1)} %copy-done.12, ...), custom_call_target="tpu_custom_call", output_to_operand_aliasing={{}: (7, {})} | custom-call | tf_op jit(solution)/shard_map/pallas_call | solution.py:229
  169.1 6.8 %shard_map.39 = bf16[1024,1664]{1,0:T(8,128)(2,1)} custom-call(s32[6]{0:T(128)} %stack.99.at_ref, bf16[64,1664]{1,0:T(8,128)(2,1)} %copy-done.15, bf16[64,1664]{1,0:T(8,128)(2,1)} %copy-done.14, bf16[64,1664]{1,0:T(8,128)(2,1)} %copy-done.17, bf16[64,1664]{1,0:T(8,128)(2,1)} %copy-done.16, ...), custom_call_target="tpu_custom_call", output_to_operand_aliasing={{}: (7, {})} | custom-call | tf_op jit(solution)/shard_map/pallas_call | solution.py:229
  (107 shorter events, 34.3 us)
Async XLA Ops:
  6.2 6.7 %collective-permute-start.2 = (bf16[208,1920]{1,0:T(8,128)(2,1)}, bf16[208,1920]{1,0:T(8,128)(2,1)S(1)}, u32[]{:S(2)}, u32[]{:S(2)}) collective-permute-start(bf16[208,1920]{1,0:T(8,128)(2,1)} %get-tuple-element.18.rest_0_), channel_id=1, source_target_pairs={{0,3},{1,2},{2,5},{3,4},{4,7},{5,6},{6,1},{7,0}} | collective-permute-start | bytes 2396168 | tf_op jit(solution)/shard_map/ppermute | solution.py:265
  29.9 7.3 %collective-permute-start.16 = (bf16[128,1664]{1,0:T(8,128)(2,1)}, bf16[128,1664]{1,0:T(8,128)(2,1)S(1)}, u32[]{:S(2)}, u32[]{:S(2)}) collective-permute-start(bf16[128,1664]{1,0:T(8,128)(2,1)} %get-tuple-element.24), channel_id=1, source_target_pairs={{0,128},{1,129},{2,130},{3,131},{4,132},{5,133},{6,134},{7,135}} | collective-permute-start | bytes 1277960 | tf_op jit(solution)/shard_map/ppermute | solution.py:319
  30.8 7.2 %collective-permute-start.17 = (bf16[128,1664]{1,0:T(8,128)(2,1)}, bf16[128,1664]{1,0:T(8,128)(2,1)S(1)}, u32[]{:S(2)}, u32[]{:S(2)}) collective-permute-start(bf16[128,1664]{1,0:T(8,128)(2,1)} %get-tuple-element.25), channel_id=1, source_target_pairs={{0,64},{1,65},{2,66},{3,67},{4,68},{5,69},{6,70},{7,71}} | collective-permute-start | bytes 1277960 | tf_op jit(solution)/shard_map/ppermute | solution.py:319
  31.5 7.2 %collective-permute-start.18 = (bf16[128,1664]{1,0:T(8,128)(2,1)}, bf16[128,1664]{1,0:T(8,128)(2,1)S(1)}, u32[]{:S(2)}, u32[]{:S(2)}) collective-permute-start(bf16[128,1664]{1,0:T(8,128)(2,1)} %get-tuple-element.26), channel_id=1, source_target_pairs={{0,192},{1,193},{2,194},{3,195},{4,196},{5,197},{6,198},{7,199}} | collective-permute-start | bytes 1277960 | tf_op jit(solution)/shard_map/ppermute | solution.py:319
  32.2 18.6 %collective-permute-start.28 = (bf16[208,1664]{1,0:T(8,128)(2,1)}, bf16[208,1664]{1,0:T(8,128)(2,1)}, u32[]{:S(2)}, u32[]{:S(2)}) collective-permute-start(bf16[208,1664]{1,0:T(8,128)(2,1)} %get-tuple-element.27), channel_id=1, source_target_pairs={{8,9},{9,8},{10,11},{11,10},{12,13},{13,12},{14,15},{15,14},{16,17... | collective-permute-start | bytes 2076680 | tf_op jit(solution)/shard_map/ppermute | solution.py:295
  40.5 18.1 %collective-permute-start.19 = (bf16[128,1664]{1,0:T(8,128)(2,1)S(1)}, bf16[128,1664]{1,0:T(8,128)(2,1)}, u32[]{:S(2)}, u32[]{:S(2)}) collective-permute-start(bf16[128,1664]{1,0:T(8,128)(2,1)S(1)} %add_select_fusion.1), channel_id=1, source_target_pairs={{0,16},{64,80},{128,144},{192,208},{1,17},{65,81},{129,145},{193,2... | collective-permute-start | bytes 1277960 | tf_op jit(solution)/shard_map/ppermute | solution.py:322
  43.0 17.5 %collective-permute-start.10 = (bf16[128,1664]{1,0:T(8,128)(2,1)S(1)}, bf16[128,1664]{1,0:T(8,128)(2,1)}, u32[]{:S(2)}, u32[]{:S(2)}) collective-permute-start(bf16[128,1664]{1,0:T(8,128)(2,1)S(1)} %add_select_fusion.3), channel_id=1, source_target_pairs={{0,16},{64,80},{128,144},{192,208},{1,17},{65,81},{129,145},{193,2... | collective-permute-start | bytes 1277960 | tf_op jit(solution)/shard_map/ppermute | solution.py:322
  44.4 16.7 %collective-permute-start.21 = (bf16[128,1664]{1,0:T(8,128)(2,1)S(1)}, bf16[128,1664]{1,0:T(8,128)(2,1)}, u32[]{:S(2)}, u32[]{:S(2)}) collective-permute-start(bf16[128,1664]{1,0:T(8,128)(2,1)S(1)} %collective-permute-done.20), channel_id=1, source_target_pairs={{48,32},{112,96},{176,160},{240,224},{49,33},{113,97},{177,161},{2... | collective-permute-start | bytes 1277960 | tf_op jit(solution)/shard_map/ppermute | solution.py:325
  52.0 13.0 %collective-permute-start.29 = (bf16[208,1664]{1,0:T(8,128)(2,1)S(1)}, bf16[208,1664]{1,0:T(8,128)(2,1)}, u32[]{:S(2)}, u32[]{:S(2)}) collective-permute-start(bf16[208,1664]{1,0:T(8,128)(2,1)S(1)} %get-tuple-element.32.rest_0_), channel_id=1, source_target_pairs={{8,10},{9,11},{10,12},{11,13},{12,14},{13,15},{14,8},{15,9},{16,18... | collective-permute-start | bytes 2076680 | tf_op jit(solution)/shard_map/ppermute | solution.py:295
  54.0 69.7 %collective-permute-start.32 = (bf16[208,1664]{1,0:T(8,128)(2,1)S(1)}, bf16[208,1664]{1,0:T(8,128)(2,1)S(1)}, u32[]{:S(2)}, u32[]{:S(2)}) collective-permute-start(bf16[208,1664]{1,0:T(8,128)(2,1)S(1)} %get-tuple-element.31.rest_1_), channel_id=1, source_target_pairs={{8,14},{9,15},{10,8},{11,9},{12,10},{13,11},{14,12},{15,13},{16,22... | collective-permute-start | bytes 2076680 | tf_op jit(solution)/shard_map/ppermute | solution.py:295
  58.5 80.4 %collective-permute-start.30 = (bf16[208,1664]{1,0:T(8,128)(2,1)S(1)}, bf16[208,1664]{1,0:T(8,128)(2,1)}, u32[]{:S(2)}, u32[]{:S(2)}) collective-permute-start(bf16[208,1664]{1,0:T(8,128)(2,1)S(1)} %get-tuple-element.31.rest_1_), channel_id=1, source_target_pairs={{8,10},{9,11},{10,12},{11,13},{12,14},{13,15},{14,8},{15,9},{16,18... | collective-permute-start | bytes 2076680 | tf_op jit(solution)/shard_map/ppermute | solution.py:295
  60.5 7.3 %collective-permute-start.11 = (bf16[128,1664]{1,0:T(8,128)(2,1)S(1)}, bf16[128,1664]{1,0:T(8,128)(2,1)S(1)}, u32[]{:S(2)}, u32[]{:S(2)}) collective-permute-start(bf16[128,1664]{1,0:T(8,128)(2,1)S(1)} %add_select_fusion.3), channel_id=1, source_target_pairs={{0,48},{64,112},{128,176},{192,240},{1,49},{65,113},{129,177},{193... | collective-permute-start | bytes 1277960 | tf_op jit(solution)/shard_map/ppermute | solution.py:323
  61.2 9.1 %collective-permute-start.12 = (bf16[128,1664]{1,0:T(8,128)(2,1)}, bf16[128,1664]{1,0:T(8,128)(2,1)S(1)}, u32[]{:S(2)}, u32[]{:S(2)}) collective-permute-start(bf16[128,1664]{1,0:T(8,128)(2,1)} %collective-permute-done.10), channel_id=1, source_target_pairs={{16,32},{80,96},{144,160},{208,224},{17,33},{81,97},{145,161},{209... | collective-permute-start | bytes 1277960 | tf_op jit(solution)/shard_map/ppermute | solution.py:325
  65.0 74.3 %collective-permute-start.31 = (bf16[208,1664]{1,0:T(8,128)(2,1)S(1)}, bf16[208,1664]{1,0:T(8,128)(2,1)}, u32[]{:S(2)}, u32[]{:S(2)}) collective-permute-start(bf16[208,1664]{1,0:T(8,128)(2,1)S(1)} %get-tuple-element.32.rest_0_), channel_id=1, source_target_pairs={{8,14},{9,15},{10,8},{11,9},{12,10},{13,11},{14,12},{15,13},{16,22... | collective-permute-start | bytes 2076680 | tf_op jit(solution)/shard_map/ppermute | solution.py:295
  67.8 71.6 %collective-permute-start.33 = (bf16[208,1664]{1,0:T(8,128)(2,1)}, bf16[208,1664]{1,0:T(8,128)(2,1)}, u32[]{:S(2)}, u32[]{:S(2)}) collective-permute-start(bf16[208,1664]{1,0:T(8,128)(2,1)} %collective-permute-done.29.rest_2_), channel_id=1, source_target_pairs={{8,10},{9,11},{10,12},{11,13},{12,14},{13,15},{14,8},{15,9},{16,18... | collective-permute-start | bytes 2076680 | tf_op jit(solution)/shard_map/ppermute | solution.py:295
  70.3 48.6 %collective-permute-start.22 = (bf16[128,1664]{1,0:T(8,128)(2,1)S(1)}, bf16[128,1664]{1,0:T(8,128)(2,1)S(1)}, u32[]{:S(2)}, u32[]{:S(2)}) collective-permute-start(bf16[128,1664]{1,0:T(8,128)(2,1)S(1)} %add_select_fusion), channel_id=1, source_target_pairs={{0,8},{16,24},{32,40},{48,56},{64,72},{80,88},{96,104},{112,120},{... | collective-permute-start | bytes 1277960 | tf_op jit(solution)/shard_map/ppermute | solution.py:328
  122.6 8.2 %collective-permute-start.23 = (bf16[128,1664]{1,0:T(8,128)(2,1)S(1)}, bf16[128,1664]{1,0:T(8,128)(2,1)S(1)}, u32[]{:S(2)}, u32[]{:S(2)}) collective-permute-start(bf16[128,1664]{1,0:T(8,128)(2,1)S(1)} %broadcast_select_fusion.2.second_ref), channel_id=1, source_target_pairs={{0,64},{16,80},{32,96},{48,112},{64,128},{80,144},{96,160},{112,17... | collective-permute-start | bytes 1277960 | tf_op jit(solution)/shard_map/ppermute | solution.py:330
  124.6 11.1 %collective-permute-start.14 = (bf16[128,1664]{1,0:T(8,128)(2,1)S(1)}, bf16[128,1664]{1,0:T(8,128)(2,1)S(1)}, u32[]{:S(2)}, u32[]{:S(2)}) collective-permute-start(bf16[128,1664]{1,0:T(8,128)(2,1)S(1)} %broadcast_select_fusion.3.first_ref), channel_id=1, source_target_pairs={{0,64},{16,80},{32,96},{48,112},{64,128},{80,144},{96,160},{112,17... | collective-permute-start | bytes 1277960 | tf_op jit(solution)/shard_map/ppermute | solution.py:330
  130.8 19.9 %collective-permute-start.34 = (bf16[208,1664]{1,0:T(8,128)(2,1)}, bf16[208,1664]{1,0:T(8,128)(2,1)}, u32[]{:S(2)}, u32[]{:S(2)}) collective-permute-start(bf16[208,1664]{1,0:T(8,128)(2,1)} %copy-done.11), channel_id=1, source_target_pairs={{8,14},{9,15},{10,8},{11,9},{12,10},{13,11},{14,12},{15,13},{16,22... | collective-permute-start | bytes 2076680 | tf_op jit(solution)/shard_map/ppermute | solution.py:295
  138.8 19.1 %collective-permute-start.36 = (bf16[128,1664]{1,0:T(8,128)(2,1)S(1)}, bf16[128,1664]{1,0:T(8,128)(2,1)S(1)}, u32[]{:S(2)}, u32[]{:S(2)}) collective-permute-start(bf16[128,1664]{1,0:T(8,128)(2,1)S(1)} %collective-permute-done.23.rest_1_), channel_id=1, source_target_pairs={{0,8},{8,0},{16,24},{24,16},{32,40},{40,32},{48,56},{56,48},{64,72... | collective-permute-start | bytes 1277960 | tf_op jit(solution)/shard_map/ppermute | solution.py:336
  139.0 18.9 %collective-permute-start.35 = (bf16[128,1664]{1,0:T(8,128)(2,1)S(1)}, bf16[128,1664]{1,0:T(8,128)(2,1)S(1)}, u32[]{:S(2)}, u32[]{:S(2)}) collective-permute-start(bf16[128,1664]{1,0:T(8,128)(2,1)S(1)} %collective-permute-done.14.rest_0_), channel_id=1, source_target_pairs={{0,8},{8,0},{16,24},{24,16},{32,40},{40,32},{48,56},{56,48},{64,72... | collective-permute-start | bytes 1277960 | tf_op jit(solution)/shard_map/ppermute | solution.py:336
  139.3 7.3 %collective-permute-start.15 = (bf16[64,1664]{1,0:T(8,128)(2,1)S(1)}, bf16[64,1664]{1,0:T(8,128)(2,1)S(1)}, u32[]{:S(2)}, u32[]{:S(2)}) collective-permute-start(bf16[64,1664]{1,0:T(8,128)(2,1)S(1)} %constant_dynamic-slice_fusion.1), channel_id=1, source_target_pairs={{0,64},{16,80},{32,96},{48,112},{64,128},{80,144},{96,160},{112,17... | collective-permute-start | bytes 638984 | tf_op jit(solution)/shard_map/ppermute | solution.py:332
  144.3 23.4 %collective-permute-start.26 = (bf16[64,1664]{1,0:T(8,128)(2,1)S(1)}, bf16[64,1664]{1,0:T(8,128)(2,1)S(1)}, u32[]{:S(2)}, u32[]{:S(2)}) collective-permute-start(bf16[64,1664]{1,0:T(8,128)(2,1)S(1)} %collective-permute-done.24.rest_1_), channel_id=1, source_target_pairs={{0,8},{8,0},{16,24},{24,16},{32,40},{40,32},{48,56},{56,48},{64,72... | collective-permute-start | bytes 638984 | tf_op jit(solution)/shard_map/ppermute | solution.py:337
  146.6 21.2 %collective-permute-start.25 = (bf16[64,1664]{1,0:T(8,128)(2,1)S(1)}, bf16[64,1664]{1,0:T(8,128)(2,1)S(1)}, u32[]{:S(2)}, u32[]{:S(2)}) collective-permute-start(bf16[64,1664]{1,0:T(8,128)(2,1)S(1)} %collective-permute-done.15.rest_0_), channel_id=1, source_target_pairs={{0,8},{8,0},{16,24},{24,16},{32,40},{40,32},{48,56},{56,48},{64,72... | collective-permute-start | bytes 638984 | tf_op jit(solution)/shard_map/ppermute | solution.py:337
  (32 other events, 375.7 us)

commit v4 on v3

--- a/solution.py
+++ b/solution.py
@@ -16,6 +16,7 @@
 ROWS_DEV = 1024
 QUARTER = 256
 FORWARD = 64
+SLABS = ((0, 512), (512, 1024), (1024, PCOLS))
 BF = jnp.bfloat16
 F32 = jnp.float32
 
@@ -200,30 +201,59 @@
     out_ref[...] = subtract(piece, factor_ref[...], weight_ref, kept_ref, at_ref[1])
 
 
+def slab_copies(factor_hbm, factor_ref, sems):
+    return [
+        pltpu.make_async_copy(factor_hbm.at[:, low:high], factor_ref.at[:, low:high], sems.at[place])
+        for place, (low, high) in enumerate(SLABS)
+    ]
+
+
+def subtract_slabs(copies, piece, factor_ref, weight_ref, kept_ref, out_ref, owner):
+    for copy, (low, high) in zip(copies, SLABS):
+        copy.wait()
+        product = jnp.dot(piece, factor_ref[:, low:high], preferred_element_type=F32)
+        trailing = (weight_ref[:, low:high].astype(F32) - product).astype(BF)
+        out_ref[:, low:high] = jnp.where(owner > 0, kept_ref[:, low:high], trailing)
+
+
 def near_kernel(at_ref, *rest):
     pieces = rest[:4]
-    factor_ref, weight_ref, kept_ref, out_ref = rest[4:]
-    for step in range(2):
-
-        @pl.when(pl.program_id(0) == step)
-        def _():
-            piece = jnp.concatenate([pieces[2 * step][...], pieces[2 * step + 1][...]], axis=0)
-            out_ref[...] = subtract(piece, factor_ref[...], weight_ref, kept_ref, at_ref[2])
+    factor_hbm, weight_ref, kept_ref, out_ref, factor_ref, sems = rest[4:]
+
+    @pl.when(pl.program_id(0) == 0)
+    def _():
+        copies = slab_copies(factor_hbm, factor_ref, sems)
+        for copy in copies:
+            copy.start()
+        piece = jnp.concatenate([pieces[0][...], pieces[1][...]], axis=0)
+        subtract_slabs(copies, piece, factor_ref, weight_ref, kept_ref, out_ref, at_ref[2])
+
+    @pl.when(pl.program_id(0) == 1)
+    def _():
+        piece = jnp.concatenate([pieces[2][...], pieces[3][...]], axis=0)
+        out_ref[...] = subtract(piece, factor_ref[...], weight_ref, kept_ref, at_ref[2])
 
 
 def far_kernel(at_ref, *rest):
     pieces = rest[:4]
-    factor_ref, weight_ref, kept_ref, out_ref, piece_ref = rest[4:]
+    factor_hbm, weight_ref, kept_ref, out_ref, factor_ref, sems, piece_ref = rest[4:]
+    copies = slab_copies(factor_hbm, factor_ref, sems)
+    for copy in copies:
+        copy.start()
     for place, part_ref in enumerate(pieces):
         start = pl.multiple_of(at_ref[2 + place] * FORWARD, FORWARD)
         piece_ref[pl.ds(start, FORWARD), :] = part_ref[...]
-    out_ref[...] = subtract(piece_ref[...], factor_ref[...], weight_ref, kept_ref, at_ref[1])
-
-
-def finish(kernel, steps, at, inputs, weight, kept, extra=None, scratch=()):
+    subtract_slabs(copies, piece_ref[...], factor_ref, weight_ref, kept_ref, out_ref, at_ref[1])
+
+
+def finish(kernel, steps, at, inputs, weight, kept, extra=None, scratch=(), slabs=False):
     block = pl.BlockSpec((QUARTER, PCOLS), lambda i, at_ref: (at_ref[i], 0))
     vmem = pl.BlockSpec(memory_space=pltpu.VMEM)
     out_shape = [jax.ShapeDtypeStruct((ROWS_DEV, PCOLS), BF)]
+    specs = [vmem] * len(inputs)
+    if slabs:
+        specs[-1] = pl.BlockSpec(memory_space=pl.ANY)
+        scratch = (pltpu.VMEM((PCOLS, PCOLS), BF), pltpu.SemaphoreType.DMA((len(SLABS),)), *scratch)
     if extra is not None:
         out_shape.append(extra)
     return pl.pallas_call(
@@ -231,7 +261,7 @@
         grid_spec=pltpu.PrefetchScalarGridSpec(
             num_scalar_prefetch=1,
             grid=(steps,),
-            in_specs=[vmem] * len(inputs) + [block, block],
+            in_specs=specs + [block, block],
             out_specs=[block] + [vmem] * (len(out_shape) - 1),
             scratch_shapes=list(scratch),
         ),
@@ -345,7 +375,7 @@
         own_kernel, 1, ints(x_at, owner, *part_rows), (*owns, token, *parts), weight, kept, factor_shape
     )
     ways = ints((x_at + 3 - 2 * core_at) % 4, (x_at + 1 + 2 * core_at) % 4, owner)
-    (out,) = finish(near_kernel, 2, ways, (*nears, *near_others, factor_all), weight, out)
+    (out,) = finish(near_kernel, 2, ways, (*nears, *near_others, factor_all), weight, out, slabs=True)
     (out,) = finish(
         far_kernel,
         1,
@@ -354,6 +384,7 @@
         weight,
         out,
         scratch=[pltpu.VMEM((QUARTER, PCOLS), BF)],
+        slabs=True,
     )
     return out
 

time: 177 us -> 178 us (level)
  no operation moved by 1% of the time
where the time goes in v4:
time: 178 us; the launch traced here: 177 us
  waiting for transfers between devices  65.7 us (37%)
  starting transfers between devices  52.7 us (30%)
  Pallas kernels  43.9 us (25%)
  local copies, waits for them, and re-layouts  6.98 us (4%)
  other arithmetic  6.53 us (4%)
    ppermute x2, waiting for transfers between devices, per_device(): shared = lax.ppermute(own, 'col', share)  48.4 us
    pallas_call x3, Pallas kernels, finish(): pl.pallas_call(kernel, grid_spec=pltpu.PrefetchScalarGridSpec(num_scalar_...  23.3 us
    ppermute x7, starting transfers between devices, along(): return lax.ppermute(array, ('col', 'row'), pairs)  22.9 us
    pallas_call x1, Pallas kernels, prune(): pl.pallas_call(prune_kernel, in_specs=[smem, smem, hbm] + [hbm] * LANES,...  15.8 us
    ppermute x7, starting transfers between devices, hop(): return lax.ppermute(array, ('col', 'row'), pairs)  7.53 us
    ppermute x7, waiting for transfers between devices, along(): return lax.ppermute(array, ('col', 'row'), pairs)  6.77 us
    pallas_call x1, Pallas kernels, local_part(): pl.pallas_call(local_kernel, in_specs=[smem, vmem], out_specs=(vmem, vmem...  4.74 us
    ppermute x2, waiting for transfers between devices, per_device(): far = lax.ppermute(onward, 'col', ring)  4.63 us
  transfers between devices with their start and end apart: 37, of which 7 were waited for; matrix products, arithmetic and copies ran while one was open for 5% of the time, Pallas kernels for 9%

profile of v4, /device:TPU:1, one launch (start us, length us, event | category | flops | bytes accessed | tf_op | source)
XLA Modules:
  0.0 176.6 jit_solution(5634597608986934945)
XLA Ops:
  0.0 4.7 %local_part.1 = (bf16[208,1920]{1,0:T(8,128)(2,1)}, bf16[208,1664]{1,0:T(8,128)(2,1)}) custom-call(s32[1]{0:T(128)} %bitcast.6.lane_ref, f32[208,1664]{1,0:T(8,128)} %factor_ref.1), custom_call_target="tpu_custom_call" | custom-call | tf_op jit(solution)/shard_map/local_part/pallas_call | solution.py:91
  7.6 1.6 collective-permute-start.4
  9.2 1.6 collective-permute-start.5
  10.8 1.6 collective-permute-start.6
  14.1 15.8 %prune.1 = (bf16[128,1664]{1,0:T(8,128)(2,1)}, bf16[128,1664]{1,0:T(8,128)(2,1)}, bf16[128,1664]{1,0:T(8,128)(2,1)}, bf16[128,1664]{1,0:T(8,128)(2,1)}, bf16[128...) custom-call(s32[8,13]{1,0:T(8,128)} %keep_ref.1, ...), custom_call_target="tpu_custom_call" | custom-call | tf_op jit(solution)/shard_map/prune/pallas_call | solution.py:173
  32.2 4.4 %collective-permute-start.28 = (bf16[208,1664]{1,0:T(8,128)(2,1)}, bf16[208,1664]{1,0:T(8,128)(2,1)}, u32[]{:S(2)}, u32[]{:S(2)}) collective-permute-start(bf16[208,1664]{1,0:T(8,128)(2,1)} %get-tuple-element.27), channel_id=1, source_target_pairs={{8,9},{9,8},{10,11},{11,10},{12,13},{13,12},{14,15},{15,14},{16,17... | collective-permute-start | bytes 2076680 | tf_op jit(solution)/shard_map/ppermute | solution.py:325
  45.9 4.9 %collective-permute-done.28 = bf16[208,1664]{1,0:T(8,128)(2,1)} collective-permute-done((bf16[208,1664]{1,0:T(8,128)(2,1)}, bf16[208,1664]{1,0:T(8,128)(2,1)}, u32[]{:S(2)}, u32[]{:S(2)}) %collective-permute-start.28) | collective-permute-done | bytes 692256 | tf_op jit(solution)/shard_map/ppermute | solution.py:325
  52.0 1.9 %collective-permute-start.29 = (bf16[208,1664]{1,0:T(8,128)(2,1)S(1)}, bf16[208,1664]{1,0:T(8,128)(2,1)}, u32[]{:S(2)}, u32[]{:S(2)}) collective-permute-start(bf16[208,1664]{1,0:T(8,128)(2,1)S(1)} %get-tuple-element.32.rest_0_), channel_id=1, source_target_pairs={{8,10},{9,11},{10,12},{11,13},{12,14},{13,15},{14,8},{15,9},{16,18... | collective-permute-start | bytes 2076680 | tf_op jit(solution)/shard_map/ppermute | solution.py:325
  54.0 4.6 %collective-permute-start.32 = (bf16[208,1664]{1,0:T(8,128)(2,1)S(1)}, bf16[208,1664]{1,0:T(8,128)(2,1)S(1)}, u32[]{:S(2)}, u32[]{:S(2)}) collective-permute-start(bf16[208,1664]{1,0:T(8,128)(2,1)S(1)} %get-tuple-element.31.rest_1_), channel_id=1, source_target_pairs={{8,14},{9,15},{10,8},{11,9},{12,10},{13,11},{14,12},{15,13},{16,22... | collective-permute-start | bytes 2076680 | tf_op jit(solution)/shard_map/ppermute | solution.py:325
  58.5 1.9 %collective-permute-start.30 = (bf16[208,1664]{1,0:T(8,128)(2,1)S(1)}, bf16[208,1664]{1,0:T(8,128)(2,1)}, u32[]{:S(2)}, u32[]{:S(2)}) collective-permute-start(bf16[208,1664]{1,0:T(8,128)(2,1)S(1)} %get-tuple-element.31.rest_1_), channel_id=1, source_target_pairs={{8,10},{9,11},{10,12},{11,13},{12,14},{13,15},{14,8},{15,9},{16,18... | collective-permute-start | bytes 2076680 | tf_op jit(solution)/shard_map/ppermute | solution.py:325
  63.2 1.9 %collective-permute-done.29.rest_2_ = bf16[208,1664]{1,0:T(8,128)(2,1)} collective-permute-done((bf16[208,1664]{1,0:T(8,128)(2,1)S(1)}, bf16[208,1664]{1,0:T(8,128)(2,1)}, u32[]{:S(2)}, u32[]{:S(2)}) %collective-permute-start.29) | collective-permute-done | bytes 692256 | tf_op jit(solution)/shard_map/ppermute | solution.py:325
  65.0 2.7 %collective-permute-start.31 = (bf16[208,1664]{1,0:T(8,128)(2,1)S(1)}, bf16[208,1664]{1,0:T(8,128)(2,1)}, u32[]{:S(2)}, u32[]{:S(2)}) collective-permute-start(bf16[208,1664]{1,0:T(8,128)(2,1)S(1)} %get-tuple-element.32.rest_0_), channel_id=1, source_target_pairs={{8,14},{9,15},{10,8},{11,9},{12,10},{13,11},{14,12},{15,13},{16,22... | collective-permute-start | bytes 2076680 | tf_op jit(solution)/shard_map/ppermute | solution.py:325
  67.8 2.6 %collective-permute-start.33 = (bf16[208,1664]{1,0:T(8,128)(2,1)}, bf16[208,1664]{1,0:T(8,128)(2,1)}, u32[]{:S(2)}, u32[]{:S(2)}) collective-permute-start(bf16[208,1664]{1,0:T(8,128)(2,1)} %collective-permute-done.29.rest_2_), channel_id=1, source_target_pairs={{8,10},{9,11},{10,12},{11,13},{12,14},{13,15},{14,8},{15,9},{16,18... | collective-permute-start | bytes 2076680 | tf_op jit(solution)/shard_map/ppermute | solution.py:325
  72.8 46.2 %collective-permute-done.22 = bf16[128,1664]{1,0:T(8,128)(2,1)S(1)} collective-permute-done((bf16[128,1664]{1,0:T(8,128)(2,1)S(1)}, bf16[128,1664]{1,0:T(8,128)(2,1)S(1)}, u32[]{:S(2)}, u32[]{:S(2)}) %collective-permute-start.22) | collective-permute-done | bytes 426016 | tf_op jit(solution)/shard_map/ppermute | solution.py:358
  120.3 2.3 %collective-permute-done.13 = bf16[128,1664]{1,0:T(8,128)(2,1)S(1)} collective-permute-done((bf16[128,1664]{1,0:T(8,128)(2,1)S(1)}, bf16[128,1664]{1,0:T(8,128)(2,1)S(1)}, u32[]{:S(2)}, u32[]{:S(2)}) %collective-permute-start.13) | collective-permute-done | bytes 426016 | tf_op jit(solution)/shard_map/ppermute | solution.py:358
  126.7 4.1 %collective-permute-done.23.rest_1_ = bf16[128,1664]{1,0:T(8,128)(2,1)S(1)} collective-permute-done((bf16[128,1664]{1,0:T(8,128)(2,1)S(1)}, bf16[128,1664]{1,0:T(8,128)(2,1)S(1)}, u32[]{:S(2)}, u32[]{:S(2)}) %collective-permute-start.23) | collective-permute-done | bytes 426016 | tf_op jit(solution)/shard_map/ppermute | solution.py:360
  130.8 4.8 %collective-permute-start.34 = (bf16[208,1664]{1,0:T(8,128)(2,1)}, bf16[208,1664]{1,0:T(8,128)(2,1)}, u32[]{:S(2)}, u32[]{:S(2)}) collective-permute-start(bf16[208,1664]{1,0:T(8,128)(2,1)} %copy-done.11), channel_id=1, source_target_pairs={{8,14},{9,15},{10,8},{11,9},{12,10},{13,11},{14,12},{15,13},{16,22... | collective-permute-start | bytes 2076680 | tf_op jit(solution)/shard_map/ppermute | solution.py:325
  137.1 1.7 collective-permute-done.27.token_ref
  139.7 4.6 %collective-permute-done.24.rest_1_ = bf16[64,1664]{1,0:T(8,128)(2,1)S(1)} collective-permute-done((bf16[64,1664]{1,0:T(8,128)(2,1)S(1)}, bf16[64,1664]{1,0:T(8,128)(2,1)S(1)}, u32[]{:S(2)}, u32[]{:S(2)}) %collective-permute-start.24) | collective-permute-done | bytes 213024 | tf_op jit(solution)/shard_map/ppermute | solution.py:362
  144.3 2.2 %collective-permute-start.26 = (bf16[64,1664]{1,0:T(8,128)(2,1)S(1)}, bf16[64,1664]{1,0:T(8,128)(2,1)S(1)}, u32[]{:S(2)}, u32[]{:S(2)}) collective-permute-start(bf16[64,1664]{1,0:T(8,128)(2,1)S(1)} %collective-permute-done.24.rest_1_), channel_id=1, source_target_pairs={{0,8},{8,0},{16,24},{24,16},{32,40},{40,32},{48,56},{56,48},{64,72... | collective-permute-start | bytes 638984 | tf_op jit(solution)/shard_map/ppermute | solution.py:367
  146.6 2.2 %collective-permute-start.25 = (bf16[64,1664]{1,0:T(8,128)(2,1)S(1)}, bf16[64,1664]{1,0:T(8,128)(2,1)S(1)}, u32[]{:S(2)}, u32[]{:S(2)}) collective-permute-start(bf16[64,1664]{1,0:T(8,128)(2,1)S(1)} %collective-permute-done.15.rest_0_), channel_id=1, source_target_pairs={{0,8},{8,0},{16,24},{24,16},{32,40},{40,32},{48,56},{56,48},{64,72... | collective-permute-start | bytes 638984 | tf_op jit(solution)/shard_map/ppermute | solution.py:367
  150.7 7.1 %shard_map.37 = (bf16[1024,1664]{1,0:T(8,128)(2,1)}, bf16[1664,1664]{1,0:T(8,128)(2,1)}) custom-call(s32[10]{0:T(128)} %stack.118.at_ref, bf16[128,1664]{1,0:T(8,128)(2,1)} %copy-done.3, bf16[128,1664]{1,0:T(8,128)(2,1)} %copy-done.2, bf16[16,128]{1,0:T(8,128)(2,1)} %copy-done.18, bf16[208,1664]{1,0:T(8,128)(2,1)} %copy-done.1, ...), custom_call_target="tpu_custom_call", output_to_operand_aliasing={{0}: (13, {})} | custom-call | tf_op jit(solution)/shard_map/pallas_call | solution.py:259
  158.8 9.2 %shard_map.38.rest_6_ = bf16[1024,1664]{1,0:T(8,128)(2,1)} custom-call(s32[3]{0:T(128)} %pad_add_fusion.at_ref, bf16[128,1664]{1,0:T(8,128)(2,1)} %copy-done.5, bf16[128,1664]{1,0:T(8,128)(2,1)} %copy-done.4, bf16[128,1664]{1,0:T(8,128)(2,1)} %copy-done.13, bf16[128,1664]{1,0:T(8,128)(2,1)} %copy-done.12, ...), custom_call_target="tpu_custom_call", output_to_operand_aliasing={{}: (7, {})} | custom-call | tf_op jit(solution)/shard_map/pallas_call | solution.py:259
  169.4 7.0 %shard_map.39 = bf16[1024,1664]{1,0:T(8,128)(2,1)} custom-call(s32[6]{0:T(128)} %stack.99.at_ref, bf16[64,1664]{1,0:T(8,128)(2,1)} %copy-done.15, bf16[64,1664]{1,0:T(8,128)(2,1)} %copy-done.14, bf16[64,1664]{1,0:T(8,128)(2,1)} %copy-done.17, bf16[64,1664]{1,0:T(8,128)(2,1)} %copy-done.16, ...), custom_call_target="tpu_custom_call", output_to_operand_aliasing={{}: (7, {})} | custom-call | tf_op jit(solution)/shard_map/pallas_call | solution.py:259
  (107 shorter events, 34.3 us)
Async XLA Ops:
  6.2 6.7 %collective-permute-start.2 = (bf16[208,1920]{1,0:T(8,128)(2,1)}, bf16[208,1920]{1,0:T(8,128)(2,1)S(1)}, u32[]{:S(2)}, u32[]{:S(2)}) collective-permute-start(bf16[208,1920]{1,0:T(8,128)(2,1)} %get-tuple-element.18.rest_0_), channel_id=1, source_target_pairs={{0,3},{1,2},{2,5},{3,4},{4,7},{5,6},{6,1},{7,0}} | collective-permute-start | bytes 2396168 | tf_op jit(solution)/shard_map/ppermute | solution.py:295
  29.9 7.3 %collective-permute-start.16 = (bf16[128,1664]{1,0:T(8,128)(2,1)}, bf16[128,1664]{1,0:T(8,128)(2,1)S(1)}, u32[]{:S(2)}, u32[]{:S(2)}) collective-permute-start(bf16[128,1664]{1,0:T(8,128)(2,1)} %get-tuple-element.24), channel_id=1, source_target_pairs={{0,128},{1,129},{2,130},{3,131},{4,132},{5,133},{6,134},{7,135}} | collective-permute-start | bytes 1277960 | tf_op jit(solution)/shard_map/ppermute | solution.py:349
  30.8 7.2 %collective-permute-start.17 = (bf16[128,1664]{1,0:T(8,128)(2,1)}, bf16[128,1664]{1,0:T(8,128)(2,1)S(1)}, u32[]{:S(2)}, u32[]{:S(2)}) collective-permute-start(bf16[128,1664]{1,0:T(8,128)(2,1)} %get-tuple-element.25), channel_id=1, source_target_pairs={{0,64},{1,65},{2,66},{3,67},{4,68},{5,69},{6,70},{7,71}} | collective-permute-start | bytes 1277960 | tf_op jit(solution)/shard_map/ppermute | solution.py:349
  31.5 7.2 %collective-permute-start.18 = (bf16[128,1664]{1,0:T(8,128)(2,1)}, bf16[128,1664]{1,0:T(8,128)(2,1)S(1)}, u32[]{:S(2)}, u32[]{:S(2)}) collective-permute-start(bf16[128,1664]{1,0:T(8,128)(2,1)} %get-tuple-element.26), channel_id=1, source_target_pairs={{0,192},{1,193},{2,194},{3,195},{4,196},{5,197},{6,198},{7,199}} | collective-permute-start | bytes 1277960 | tf_op jit(solution)/shard_map/ppermute | solution.py:349
  32.2 18.6 %collective-permute-start.28 = (bf16[208,1664]{1,0:T(8,128)(2,1)}, bf16[208,1664]{1,0:T(8,128)(2,1)}, u32[]{:S(2)}, u32[]{:S(2)}) collective-permute-start(bf16[208,1664]{1,0:T(8,128)(2,1)} %get-tuple-element.27), channel_id=1, source_target_pairs={{8,9},{9,8},{10,11},{11,10},{12,13},{13,12},{14,15},{15,14},{16,17... | collective-permute-start | bytes 2076680 | tf_op jit(solution)/shard_map/ppermute | solution.py:325
  40.5 18.1 %collective-permute-start.19 = (bf16[128,1664]{1,0:T(8,128)(2,1)S(1)}, bf16[128,1664]{1,0:T(8,128)(2,1)}, u32[]{:S(2)}, u32[]{:S(2)}) collective-permute-start(bf16[128,1664]{1,0:T(8,128)(2,1)S(1)} %add_select_fusion.1), channel_id=1, source_target_pairs={{0,16},{64,80},{128,144},{192,208},{1,17},{65,81},{129,145},{193,2... | collective-permute-start | bytes 1277960 | tf_op jit(solution)/shard_map/ppermute | solution.py:352
  43.0 17.5 %collective-permute-start.10 = (bf16[128,1664]{1,0:T(8,128)(2,1)S(1)}, bf16[128,1664]{1,0:T(8,128)(2,1)}, u32[]{:S(2)}, u32[]{:S(2)}) collective-permute-start(bf16[128,1664]{1,0:T(8,128)(2,1)S(1)} %add_select_fusion.3), channel_id=1, source_target_pairs={{0,16},{64,80},{128,144},{192,208},{1,17},{65,81},{129,145},{193,2... | collective-permute-start | bytes 1277960 | tf_op jit(solution)/shard_map/ppermute | solution.py:352
  44.4 16.7 %collective-permute-start.21 = (bf16[128,1664]{1,0:T(8,128)(2,1)S(1)}, bf16[128,1664]{1,0:T(8,128)(2,1)}, u32[]{:S(2)}, u32[]{:S(2)}) collective-permute-start(bf16[128,1664]{1,0:T(8,128)(2,1)S(1)} %collective-permute-done.20), channel_id=1, source_target_pairs={{48,32},{112,96},{176,160},{240,224},{49,33},{113,97},{177,161},{2... | collective-permute-start | bytes 1277960 | tf_op jit(solution)/shard_map/ppermute | solution.py:355
  52.0 13.0 %collective-permute-start.29 = (bf16[208,1664]{1,0:T(8,128)(2,1)S(1)}, bf16[208,1664]{1,0:T(8,128)(2,1)}, u32[]{:S(2)}, u32[]{:S(2)}) collective-permute-start(bf16[208,1664]{1,0:T(8,128)(2,1)S(1)} %get-tuple-element.32.rest_0_), channel_id=1, source_target_pairs={{8,10},{9,11},{10,12},{11,13},{12,14},{13,15},{14,8},{15,9},{16,18... | collective-permute-start | bytes 2076680 | tf_op jit(solution)/shard_map/ppermute | solution.py:325
  54.0 69.7 %collective-permute-start.32 = (bf16[208,1664]{1,0:T(8,128)(2,1)S(1)}, bf16[208,1664]{1,0:T(8,128)(2,1)S(1)}, u32[]{:S(2)}, u32[]{:S(2)}) collective-permute-start(bf16[208,1664]{1,0:T(8,128)(2,1)S(1)} %get-tuple-element.31.rest_1_), channel_id=1, source_target_pairs={{8,14},{9,15},{10,8},{11,9},{12,10},{13,11},{14,12},{15,13},{16,22... | collective-permute-start | bytes 2076680 | tf_op jit(solution)/shard_map/ppermute | solution.py:325
  58.5 80.4 %collective-permute-start.30 = (bf16[208,1664]{1,0:T(8,128)(2,1)S(1)}, bf16[208,1664]{1,0:T(8,128)(2,1)}, u32[]{:S(2)}, u32[]{:S(2)}) collective-permute-start(bf16[208,1664]{1,0:T(8,128)(2,1)S(1)} %get-tuple-element.31.rest_1_), channel_id=1, source_target_pairs={{8,10},{9,11},{10,12},{11,13},{12,14},{13,15},{14,8},{15,9},{16,18... | collective-permute-start | bytes 2076680 | tf_op jit(solution)/shard_map/ppermute | solution.py:325
  60.5 7.3 %collective-permute-start.11 = (bf16[128,1664]{1,0:T(8,128)(2,1)S(1)}, bf16[128,1664]{1,0:T(8,128)(2,1)S(1)}, u32[]{:S(2)}, u32[]{:S(2)}) collective-permute-start(bf16[128,1664]{1,0:T(8,128)(2,1)S(1)} %add_select_fusion.3), channel_id=1, source_target_pairs={{0,48},{64,112},{128,176},{192,240},{1,49},{65,113},{129,177},{193... | collective-permute-start | bytes 1277960 | tf_op jit(solution)/shard_map/ppermute | solution.py:353
  61.2 9.1 %collective-permute-start.12 = (bf16[128,1664]{1,0:T(8,128)(2,1)}, bf16[128,1664]{1,0:T(8,128)(2,1)S(1)}, u32[]{:S(2)}, u32[]{:S(2)}) collective-permute-start(bf16[128,1664]{1,0:T(8,128)(2,1)} %collective-permute-done.10), channel_id=1, source_target_pairs={{16,32},{80,96},{144,160},{208,224},{17,33},{81,97},{145,161},{209... | collective-permute-start | bytes 1277960 | tf_op jit(solution)/shard_map/ppermute | solution.py:355
  65.0 74.3 %collective-permute-start.31 = (bf16[208,1664]{1,0:T(8,128)(2,1)S(1)}, bf16[208,1664]{1,0:T(8,128)(2,1)}, u32[]{:S(2)}, u32[]{:S(2)}) collective-permute-start(bf16[208,1664]{1,0:T(8,128)(2,1)S(1)} %get-tuple-element.32.rest_0_), channel_id=1, source_target_pairs={{8,14},{9,15},{10,8},{11,9},{12,10},{13,11},{14,12},{15,13},{16,22... | collective-permute-start | bytes 2076680 | tf_op jit(solution)/shard_map/ppermute | solution.py:325
  67.8 71.6 %collective-permute-start.33 = (bf16[208,1664]{1,0:T(8,128)(2,1)}, bf16[208,1664]{1,0:T(8,128)(2,1)}, u32[]{:S(2)}, u32[]{:S(2)}) collective-permute-start(bf16[208,1664]{1,0:T(8,128)(2,1)} %collective-permute-done.29.rest_2_), channel_id=1, source_target_pairs={{8,10},{9,11},{10,12},{11,13},{12,14},{13,15},{14,8},{15,9},{16,18... | collective-permute-start | bytes 2076680 | tf_op jit(solution)/shard_map/ppermute | solution.py:325
  70.3 48.6 %collective-permute-start.22 = (bf16[128,1664]{1,0:T(8,128)(2,1)S(1)}, bf16[128,1664]{1,0:T(8,128)(2,1)S(1)}, u32[]{:S(2)}, u32[]{:S(2)}) collective-permute-start(bf16[128,1664]{1,0:T(8,128)(2,1)S(1)} %add_select_fusion), channel_id=1, source_target_pairs={{0,8},{16,24},{32,40},{48,56},{64,72},{80,88},{96,104},{112,120},{... | collective-permute-start | bytes 1277960 | tf_op jit(solution)/shard_map/ppermute | solution.py:358
  122.6 8.2 %collective-permute-start.23 = (bf16[128,1664]{1,0:T(8,128)(2,1)S(1)}, bf16[128,1664]{1,0:T(8,128)(2,1)S(1)}, u32[]{:S(2)}, u32[]{:S(2)}) collective-permute-start(bf16[128,1664]{1,0:T(8,128)(2,1)S(1)} %broadcast_select_fusion.2.second_ref), channel_id=1, source_target_pairs={{0,64},{16,80},{32,96},{48,112},{64,128},{80,144},{96,160},{112,17... | collective-permute-start | bytes 1277960 | tf_op jit(solution)/shard_map/ppermute | solution.py:360
  124.6 11.1 %collective-permute-start.14 = (bf16[128,1664]{1,0:T(8,128)(2,1)S(1)}, bf16[128,1664]{1,0:T(8,128)(2,1)S(1)}, u32[]{:S(2)}, u32[]{:S(2)}) collective-permute-start(bf16[128,1664]{1,0:T(8,128)(2,1)S(1)} %broadcast_select_fusion.3.first_ref), channel_id=1, source_target_pairs={{0,64},{16,80},{32,96},{48,112},{64,128},{80,144},{96,160},{112,17... | collective-permute-start | bytes 1277960 | tf_op jit(solution)/shard_map/ppermute | solution.py:360
  130.8 19.9 %collective-permute-start.34 = (bf16[208,1664]{1,0:T(8,128)(2,1)}, bf16[208,1664]{1,0:T(8,128)(2,1)}, u32[]{:S(2)}, u32[]{:S(2)}) collective-permute-start(bf16[208,1664]{1,0:T(8,128)(2,1)} %copy-done.11), channel_id=1, source_target_pairs={{8,14},{9,15},{10,8},{11,9},{12,10},{13,11},{14,12},{15,13},{16,22... | collective-permute-start | bytes 2076680 | tf_op jit(solution)/shard_map/ppermute | solution.py:325
  138.8 19.1 %collective-permute-start.36 = (bf16[128,1664]{1,0:T(8,128)(2,1)S(1)}, bf16[128,1664]{1,0:T(8,128)(2,1)S(1)}, u32[]{:S(2)}, u32[]{:S(2)}) collective-permute-start(bf16[128,1664]{1,0:T(8,128)(2,1)S(1)} %collective-permute-done.23.rest_1_), channel_id=1, source_target_pairs={{0,8},{8,0},{16,24},{24,16},{32,40},{40,32},{48,56},{56,48},{64,72... | collective-permute-start | bytes 1277960 | tf_op jit(solution)/shard_map/ppermute | solution.py:366
  139.0 18.9 %collective-permute-start.35 = (bf16[128,1664]{1,0:T(8,128)(2,1)S(1)}, bf16[128,1664]{1,0:T(8,128)(2,1)S(1)}, u32[]{:S(2)}, u32[]{:S(2)}) collective-permute-start(bf16[128,1664]{1,0:T(8,128)(2,1)S(1)} %collective-permute-done.14.rest_0_), channel_id=1, source_target_pairs={{0,8},{8,0},{16,24},{24,16},{32,40},{40,32},{48,56},{56,48},{64,72... | collective-permute-start | bytes 1277960 | tf_op jit(solution)/shard_map/ppermute | solution.py:366
  139.3 7.3 %collective-permute-start.15 = (bf16[64,1664]{1,0:T(8,128)(2,1)S(1)}, bf16[64,1664]{1,0:T(8,128)(2,1)S(1)}, u32[]{:S(2)}, u32[]{:S(2)}) collective-permute-start(bf16[64,1664]{1,0:T(8,128)(2,1)S(1)} %constant_dynamic-slice_fusion.1), channel_id=1, source_target_pairs={{0,64},{16,80},{32,96},{48,112},{64,128},{80,144},{96,160},{112,17... | collective-permute-start | bytes 638984 | tf_op jit(solution)/shard_map/ppermute | solution.py:362
  144.3 23.7 %collective-permute-start.26 = (bf16[64,1664]{1,0:T(8,128)(2,1)S(1)}, bf16[64,1664]{1,0:T(8,128)(2,1)S(1)}, u32[]{:S(2)}, u32[]{:S(2)}) collective-permute-start(bf16[64,1664]{1,0:T(8,128)(2,1)S(1)} %collective-permute-done.24.rest_1_), channel_id=1, source_target_pairs={{0,8},{8,0},{16,24},{24,16},{32,40},{40,32},{48,56},{56,48},{64,72... | collective-permute-start | bytes 638984 | tf_op jit(solution)/shard_map/ppermute | solution.py:367
  146.6 21.5 %collective-permute-start.25 = (bf16[64,1664]{1,0:T(8,128)(2,1)S(1)}, bf16[64,1664]{1,0:T(8,128)(2,1)S(1)}, u32[]{:S(2)}, u32[]{:S(2)}) collective-permute-start(bf16[64,1664]{1,0:T(8,128)(2,1)S(1)} %collective-permute-done.15.rest_0_), channel_id=1, source_target_pairs={{0,8},{8,0},{16,24},{24,16},{32,40},{40,32},{48,56},{56,48},{64,72... | collective-permute-start | bytes 638984 | tf_op jit(solution)/shard_map/ppermute | solution.py:367
  (32 other events, 375.7 us)
